TPU v7x, 32 devices: a whole 2x2x4 slice. The times are simulated.
32 devices in a mesh: dp: 8 (over y, x, core), tensor: 4 (over z).
Axes of the slice: x: 2, y: 2, z: 4, core: 2. Of those that a mesh axis runs over, the one named last changes fastest.
Arguments:
- norm_input: bfloat16 [16384, 8192], P(('dp', 'tensor')), may hold values from -6 to 6
- key_grad: bfloat16 [16384, 512], P(('dp', 'tensor')), may hold values from -100 to 100
- positions: int32 [16384], P(('dp', 'tensor')), may hold values from 0 to 8191
- norm_gain: bfloat16 [8192], replicated, may hold values from 0.25 to 1.75
- key_weight: bfloat16 [512, 8192], P('dp', 'tensor'), may hold values from -0.0625 to 0.0625
- first_moment: float32 [512, 8192], P('dp', 'tensor'), may hold values from -6 to 6
- second_moment: float32 [512, 8192], P('dp', 'tensor'), may hold values from 0.1 to 4
Outputs:
- input_grad: bfloat16 [16384, 8192], P(('dp', 'tensor'))
- new_weight: bfloat16 [512, 8192], P(None, 'tensor')
- new_first: float32 [512, 8192], P('dp', 'tensor')
- new_second: float32 [512, 8192], P('dp', 'tensor')
All inputs are finite; a program needn't handle non-finite values.
Results may differ from a plain program's by a relative error of at most 0.01.
Values may be sent and summed in bfloat16 or wider, within the bound.
A program may use at most 128 MiB of HBM per device.

v0:
```python
import functools
import math

import jax
import jax.numpy as jnp
from jax import lax
from jax.experimental import pallas as pl
from jax.experimental.pallas import tpu as pltpu
from jax.sharding import PartitionSpec as P

KV_HEADS = 4
HEAD = 128


eps_norm = 1e-05
beta_one = 0.9
beta_two = 0.95
learn_rate = 0.0003
decay_rate = 0.1
eps_adam = 1e-08


def unrotate(incoming, positions):
    row_count = incoming.shape[0]
    half_width = HEAD // 2
    frequency = 500000.0 ** (-(2.0 * jnp.arange(half_width, dtype=jnp.float32)) / HEAD)
    angles = positions.astype(jnp.float32)[:, None] * frequency[None, :]
    cosine = jnp.cos(angles)[:, None, :]
    sine_table = jnp.sin(angles)[:, None, :]
    pieces = incoming.astype(jnp.float32).reshape(row_count, KV_HEADS, 2, half_width)
    first_half = pieces[:, :, 0, :]
    second_half = pieces[:, :, 1, :]
    upper_part = first_half * cosine + second_half * sine_table
    lower_part = second_half * cosine - first_half * sine_table
    return (
        jnp.stack([upper_part, lower_part], axis=2)
        .reshape(row_count, KV_HEADS * HEAD)
        .astype(jnp.bfloat16)
    )


MESH = pl.DeviceIdType.MESH
F32 = jnp.float32
BF16 = jnp.bfloat16


def kernel(
    ndp, nt, nqx, x_hbm, kb, kbt, gain, w, m1, m2,
    ig_hbm, nw_hbm, nf, ns,
    x, normed, wf, wg, rcore, r1a, r1b, r2a, r2b, zs, rz, gsum, sinv, cross, nwb, nsend, nrecv,
    lsem, xsem, osem, a1s, a1r, a2s, a2r, a3s, a3r, b3s, b3r, cs, cr, qs, qr, q2s, q2r,
    zsd, zr, nss, nsr, ws, wr, vs, vr,
):
    nq = ndp // 2
    nqy = nq // nqx
    rows, cols = w.shape
    half = nq * rows
    tokens, width = x.shape
    tile = min(128, tokens)
    ntile = tokens // tile
    cc = min(512, cols)
    hc = cols // 2
    ha = pl.ds(0, hc)
    hb = pl.ds(hc, hc)
    dp = lax.axis_index("dp")
    t = lax.axis_index("tensor")
    c = dp % 2
    q = dp // 2
    qy = q // nqx
    qx = q % nqx
    mate = q * 2 + (1 - c)
    mine = pl.multiple_of(c * half, half)
    theirs = pl.multiple_of((1 - c) * half, half)
    sends = []

    def remote(src, dst, ssem, rsem, dev):
        copy = pltpu.make_async_remote_copy(
            src_ref=src, dst_ref=dst, send_sem=ssem, recv_sem=rsem, device_id=dev, device_id_type=MESH
        )
        copy.start()
        sends.append(copy)
        return copy

    def pos_x(k):
        return (qx + k) % nqx

    def pos_y(k):
        return (qy + k) % nqy

    def dev_x(k):
        return ((qy * nqx + pos_x(k)) * 2 + c, t)

    def dev_y(k):
        return ((pos_y(k) * nqx + qx) * 2 + c, t)

    def slot(yy, xx):
        return pl.ds(pl.multiple_of(mine + (yy * nqx + xx) * rows, rows), rows)

    def peer_t(i):
        return (t + 1 + i) % nt

    x_in = []
    for k in range(ntile):
        piece = pl.ds(k * tile, tile)
        copy = pltpu.make_async_copy(x_hbm.at[piece], x.at[piece], xsem.at[k])
        copy.start()
        x_in.append(copy)
    my_rows = slot(qy, qx)
    own = pltpu.make_async_copy(w, wf.at[t, my_rows], lsem)
    own.start()

    barrier = pltpu.get_barrier_semaphore()
    pl.semaphore_signal(barrier, inc=1, device_id=(mate, t), device_id_type=MESH)
    for k in range(1, nqx):
        pl.semaphore_signal(barrier, inc=1, device_id=dev_x(k), device_id_type=MESH)
    for k in range(1, nqy):
        pl.semaphore_signal(barrier, inc=1, device_id=dev_y(k), device_id_type=MESH)
    for i in range(nt - 1):
        pl.semaphore_signal(barrier, inc=1, device_id=(dp, peer_t(i)), device_id_type=MESH)
    pl.semaphore_wait(barrier, 1 + (nqx - 1) + (nqy - 1) + (nt - 1))

    a1 = [remote(w, wf.at[t, my_rows], a1s.at[i], a1r.at[i], (dp, peer_t(i))) for i in range(nt - 1)]
    na = nqx + nqy - 2
    first_hop = {}
    second_hop = {}

    def block(i):
        return (t + nt - i) % nt

    def gather_first(i):
        j = block(i)
        if i > 0:
            a1[i - 1].wait_recv()
        src = w if i == 0 else wf.at[j, my_rows]
        batch = []
        for k in range(1, nqx):
            n = i * na + k - 1
            batch.append(
                remote(src.at[:, ha], wf.at[j, my_rows, ha], a2s.at[n], a2r.at[n], dev_x(k))
            )
        for k in range(1, nqy):
            n = i * na + nqx - 1 + k - 1
            batch.append(
                remote(src.at[:, hb], wf.at[j, my_rows, hb], a2s.at[n], a2r.at[n], dev_y(k))
            )
        first_hop[i] = batch

    nb = (nqx - 1) * nqy + (nqy - 1) * nqx

    def gather_second(i):
        j = block(i)
        for copy in first_hop[i]:
            copy.wait_recv()
        batch = []
        n = i * nb
        for k in range(1, nqy):
            for xx in range(nqx):
                part = wf.at[j, slot(qy, xx), ha]
                batch.append(remote(part, part, b3s.at[n], b3r.at[n], dev_y(k)))
                n += 1
        for k in range(1, nqx):
            for yy in range(nqy):
                part = wf.at[j, slot(yy, qx), hb]
                batch.append(remote(part, part, b3s.at[n], b3r.at[n], dev_x(k)))
                n += 1
        second_hop[i] = batch

    gather_first(0)
    cross[...] = jnp.zeros_like(cross)

    for k in range(ntile):
        x_in[k].wait()

        @pl.loop(0, tile // 16)
        def _(g):
            r = pl.ds(pl.multiple_of(k * tile + g * 16, 16), 16)
            v = x[r, :].astype(F32)
            s = lax.rsqrt(jnp.sum(v * v, axis=1, keepdims=True) / width + eps_norm)
            sinv[r, :] = jnp.broadcast_to(s, (16, 128))
            normed[r, :] = (v * s * gain[...]).astype(BF16)

        if k == ntile // 2:
            own.wait()
            gather_second(0)
        if k == ntile - 1:
            gather_first(1)

    def product(j):
        @pl.loop(0, cols // cc)
        def _(h):
            off = pl.multiple_of(h * cc, cc)
            col = pl.ds(pl.multiple_of(j * cols + h * cc, cc), cc)
            wg[j, :, pl.ds(off, cc)] = jnp.dot(
                kbt[...], normed[:, col], preferred_element_type=F32
            ).astype(BF16)

    core_copies = []
    q_copies = []
    q2_copies = []

    def pair_sum(i):
        j = peer_t(i)
        core_copies[i].wait_recv()

        @pl.loop(0, half // 16)
        def _(g):
            r = pl.ds(pl.multiple_of(mine + g * 16, 16), 16)
            a = wg[j, r, :].astype(F32) + rcore[j, pl.ds(pl.multiple_of(g * 16, 16), 16), :].astype(F32)
            wg[j, r, :] = a.astype(BF16)

        batch = []
        n = i * nb
        for k in range(1, nqx):
            for yy in range(nqy):
                src = wg.at[j, slot(yy, pos_x(k)), ha]
                batch.append(
                    remote(src, r1a.at[i, (k - 1) * nqy + yy], qs.at[n], qr.at[n], dev_x(k))
                )
                n += 1
        for k in range(1, nqy):
            for xx in range(nqx):
                src = wg.at[j, slot(pos_y(k), xx), hb]
                batch.append(
                    remote(src, r1b.at[i, (k - 1) * nqx + xx], qs.at[n], qr.at[n], dev_y(k))
                )
                n += 1
        q_copies.append(batch)

    for i in range(nt):
        j = peer_t(i)
        product(j)
        core_copies.append(
            remote(wg.at[j, pl.ds(theirs, half)], rcore.at[j], cs.at[i], cr.at[i], (mate, t))
        )
        if i == 1:
            gather_second(1)
        if i > 0:
            pair_sum(i - 1)
    pair_sum(nt - 1)

    def middle(i):
        j = peer_t(i)
        for copy in q_copies[i]:
            copy.wait_recv()

        @pl.loop(0, rows // 16)
        def _(g):
            l = pl.ds(pl.multiple_of(g * 16, 16), 16)
            for yy in range(nqy):
                r = pl.ds(pl.multiple_of(mine + (yy * nqx + qx) * rows + g * 16, 16), 16)
                a = wg[j, r, ha].astype(F32)
                for k in range(nqx - 1):
                    a = a + r1a[i, k * nqy + yy, l, :].astype(F32)
                wg[j, r, ha] = a.astype(BF16)
            for xx in range(nqx):
                r = pl.ds(pl.multiple_of(mine + (qy * nqx + xx) * rows + g * 16, 16), 16)
                a = wg[j, r, hb].astype(F32)
                for k in range(nqy - 1):
                    a = a + r1b[i, k * nqx + xx, l, :].astype(F32)
                wg[j, r, hb] = a.astype(BF16)

        batch = []
        n = i * na
        for k in range(1, nqy):
            batch.append(
                remote(wg.at[j, slot(pos_y(k), qx), ha], r2a.at[i, k - 1], q2s.at[n], q2r.at[n], dev_y(k))
            )
            n += 1
        for k in range(1, nqx):
            batch.append(
                remote(wg.at[j, slot(qy, pos_x(k)), hb], r2b.at[i, k - 1], q2s.at[n], q2r.at[n], dev_x(k))
            )
            n += 1
        q2_copies.append(batch)

    z_copies = []

    def final(i):
        j = peer_t(i)
        for copy in q2_copies[i]:
            copy.wait_recv()

        @pl.loop(0, rows // 16)
        def _(g):
            r = pl.ds(pl.multiple_of(g * 16, 16), 16)
            m = pl.ds(pl.multiple_of(mine + q * rows + g * 16, 16), 16)
            for part, other, count in ((ha, r2a, nqy - 1), (hb, r2b, nqx - 1)):
                a = wg[j, m, part].astype(F32)
                for k in range(count):
                    a = a + other[i, k, r, :].astype(F32)
                if i < nt - 1:
                    zs[i, r, part] = a.astype(BF16)
                else:
                    gsum[r, part] = a

        if i < nt - 1:
            z_copies.append(remote(zs.at[i], rz.at[i], zsd.at[i], zr.at[i], (dp, j)))

    for i in range(nt):
        middle(i)
        if i > 1:
            gather_first(i)
    for i in range(nt):
        final(i)
        if i > 1:
            gather_second(i)

    a3 = {}

    def gather_third(i):
        for copy in second_hop[i]:
            copy.wait_recv()
        part = wf.at[block(i), pl.ds(mine, half)]
        a3[i] = remote(part, part, a3s.at[i], a3r.at[i], (mate, t))

    uc = min(256, cols)

    def upstream(i):
        j = block(i)
        a3[i].wait_recv()

        @pl.loop(0, cols // uc)
        def _(h):
            off = pl.ds(pl.multiple_of(h * uc, uc), uc)
            col = pl.ds(pl.multiple_of(j * cols + h * uc, uc), uc)
            u = jnp.dot(kb[...], wf[j, :, off], preferred_element_type=F32) * gain[:, col]
            normed[:, col] = u.astype(BF16)
            p = u * x[:, col].astype(F32)
            total = p[:, :128]
            for b in range(1, uc // 128):
                total = total + p[:, b * 128 : (b + 1) * 128]
            cross[...] += total

    for i in range(2):
        gather_third(i)
        upstream(i)
    for copy in z_copies:
        copy.wait_recv()

    nsend[0] = jnp.zeros((8, 128), F32)

    @pl.loop(0, rows // 16)
    def _(g):
        r = pl.ds(pl.multiple_of(g * 16, 16), 16)
        a = gsum[r, :]
        for i in range(nt - 1):
            a = a + rz[i, r, :].astype(F32)
        gsum[r, :] = a
        a = a * a
        a = a[:8] + a[8:]
        total = a[:, :128]
        for k in range(1, cols // 128):
            total = total + a[:, k * 128 : (k + 1) * 128]
        nsend[0] += total

    base = 0
    v = nsend[0]
    groups = (
        [(mate, t)],
        [(dp, peer_t(i)) for i in range(nt - 1)],
        [dev_x(k) for k in range(1, nqx)],
        [dev_y(k) for k in range(1, nqy)],
    )
    for step, devs in enumerate(groups):
        if step > 0:
            nsend[step] = v
        batch = [
            remote(nsend.at[step], nrecv.at[base + n], nss.at[base + n], nsr.at[base + n], dev)
            for n, dev in enumerate(devs)
        ]
        if step == 1:
            for i in range(2, nt - 1):
                gather_third(i)
                upstream(i)
        for n, copy in enumerate(batch):
            copy.wait_recv()
            v = v + nrecv[base + n]
        base += len(devs)
    total_square = jnp.sum(jnp.sum(v, axis=1, keepdims=True), axis=0, keepdims=True)
    limit = math.sqrt(kbt.shape[0] * width)
    clip = jnp.minimum(1.0, limit / (jnp.sqrt(total_square) + 1e-06))
    nat = pl.multiple_of(c * rows, rows)

    @pl.loop(0, rows // 16)
    def _(g):
        r = pl.ds(pl.multiple_of(g * 16, 16), 16)
        clipped = gsum[r, :] * clip
        first = beta_one * m1[r, :] + (1.0 - beta_one) * clipped
        second = beta_two * m2[r, :] + (1.0 - beta_two) * clipped * clipped
        nf[r, :] = first
        ns[r, :] = second
        nwb[q, pl.ds(pl.multiple_of(nat + g * 16, 16), 16), :] = (
            w[r, :].astype(F32) * (1.0 - learn_rate * decay_rate)
            - learn_rate * first / (jnp.sqrt(second) + eps_adam)
        ).astype(BF16)

    def piece_of(yy, xx, part):
        return nwb.at[yy * nqx + xx, pl.ds(nat, rows), part]

    w_first = []
    for k in range(1, nqx):
        part = piece_of(qy, qx, ha)
        w_first.append(remote(part, part, ws.at[k - 1], wr.at[k - 1], dev_x(k)))
    for k in range(1, nqy):
        n = nqx - 1 + k - 1
        part = piece_of(qy, qx, hb)
        w_first.append(remote(part, part, ws.at[n], wr.at[n], dev_y(k)))

    gather_third(nt - 1)
    upstream(nt - 1)

    for copy in w_first:
        copy.wait_recv()
    w_second = []
    for k in range(1, nqy):
        for xx in range(nqx):
            part = piece_of(qy, xx, ha)
            n = len(w_second)
            w_second.append(remote(part, part, vs.at[n], vr.at[n], dev_y(k)))
    for k in range(1, nqx):
        for yy in range(nqy):
            part = piece_of(yy, qx, hb)
            n = len(w_second)
            w_second.append(remote(part, part, vs.at[n], vr.at[n], dev_x(k)))

    outs = []
    for k in range(ntile):
        piece = pl.ds(k * tile, tile)

        @pl.loop(0, tile // 16)
        def _(g):
            r = pl.ds(pl.multiple_of(k * tile + g * 16, 16), 16)
            s = sinv[r, :1]
            inner = s * (jnp.sum(cross[r, :], axis=1, keepdims=True) / width)
            normed[r, :] = (
                s * (normed[r, :].astype(F32) - x[r, :].astype(F32) * s * inner)
            ).astype(BF16)

        copy = pltpu.make_async_copy(normed.at[piece], ig_hbm.at[piece], osem.at[k])
        copy.start()
        outs.append(copy)

    for copy in w_second:
        copy.wait_recv()
    part = nwb.at[:, pl.ds(nat, rows)]
    last = remote(part, part, vs.at[nb], vr.at[nb], (mate, t))
    last.wait_recv()
    copy = pltpu.make_async_copy(nwb, nw_hbm, lsem)
    copy.start()
    for copy_out in outs:
        copy_out.wait()
    for sent in sends:
        sent.wait_send()
    copy.wait()


def body(ndp, nt, norm_input, key_grad, positions, norm_gain, key_weight, first_moment, second_moment):
    rows, cols = key_weight.shape
    tokens, width = norm_input.shape
    nq = ndp // 2
    features = ndp * rows
    back = unrotate(key_grad, positions)
    back = back.reshape(tokens, nq, 2, rows).transpose(0, 2, 1, 3).reshape(tokens, features)
    tile = min(128, tokens)
    ntile = tokens // tile
    any_spec = pl.BlockSpec(memory_space=pl.ANY)
    vmem = pl.BlockSpec(memory_space=pltpu.VMEM)
    dma = pltpu.SemaphoreType.DMA
    nqx = math.isqrt(nq)
    while nq % nqx:
        nqx -= 1
    nqy = nq // nqx
    hc = cols // 2
    na = nqx + nqy - 2
    nb = (nqx - 1) * nqy + (nqy - 1) * nqx
    nn = 1 + na + nt - 1
    scratch = [
        pltpu.VMEM((tokens, width), BF16),
        pltpu.VMEM((tokens, width), BF16),
        pltpu.VMEM((nt, features, cols), BF16),
        pltpu.VMEM((nt, features, cols), BF16),
        pltpu.VMEM((nt, nq * rows, cols), BF16),
        pltpu.VMEM((nt, (nqx - 1) * nqy, rows, hc), BF16),
        pltpu.VMEM((nt, (nqy - 1) * nqx, rows, hc), BF16),
        pltpu.VMEM((nt, nqy - 1, rows, hc), BF16),
        pltpu.VMEM((nt, nqx - 1, rows, hc), BF16),
        pltpu.VMEM((nt - 1, rows, cols), BF16),
        pltpu.VMEM((nt - 1, rows, cols), BF16),
        pltpu.VMEM((rows, cols), F32),
        pltpu.VMEM((tokens, 128), F32),
        pltpu.VMEM((tokens, 128), F32),
        pltpu.VMEM((nq, 2 * rows, cols), BF16),
        pltpu.VMEM((4, 8, 128), F32),
        pltpu.VMEM((nn, 8, 128), F32),
        dma, dma((ntile,)), dma((ntile,)),
    ]
    for count in (nt - 1, nt * na, nt, nt * nb, nt, nt * nb, nt * na, nt - 1, nn, na, nb + 1):
        scratch += [dma((count,)), dma((count,))]
    input_grad, new_weight, new_first, new_second = pl.pallas_call(
        functools.partial(kernel, ndp, nt, nqx),
        out_shape=(
            jax.ShapeDtypeStruct((tokens, width), BF16),
            jax.ShapeDtypeStruct((nq, 2 * rows, cols), BF16),
            jax.ShapeDtypeStruct((rows, cols), F32),
            jax.ShapeDtypeStruct((rows, cols), F32),
        ),
        in_specs=[any_spec] + [vmem] * 6,
        out_specs=(any_spec, any_spec, vmem, vmem),
        scratch_shapes=scratch,
        compiler_params=pltpu.CompilerParams(
            collective_id=0, has_side_effects=True, vmem_limit_bytes=62 * 2**20
        ),
    )(
        norm_input, back, back.T, norm_gain.astype(F32)[None, :], key_weight, first_moment, second_moment,
    )
    return (input_grad, new_weight.reshape(features, cols), new_first, new_second)


def solution(mesh):
    in_specs = (
        P(("dp", "tensor"), None),
        P(("dp", "tensor"), None),
        P(("dp", "tensor")),
        P(),
        P("dp", "tensor"),
        P("dp", "tensor"),
        P("dp", "tensor"),
    )
    out_specs = (P(("dp", "tensor"), None), P(None, "tensor"), P("dp", "tensor"), P("dp", "tensor"))
    return jax.shard_map(
        functools.partial(body, mesh.shape["dp"], mesh.shape["tensor"]),
        mesh=mesh, in_specs=in_specs, out_specs=out_specs, check_vma=False,
    )
```

profile of v0, /device:TPU:0, one launch (start us, length us, event | category | flops | bytes accessed | tf_op | source)
XLA Modules:
  0.0 133.4 jit_solution(10907808466328008786)
XLA Ops:
  0.6 0.7 convert_element_type.3
  1.3 1.3 broadcast_in_dim.11
  2.7 0.5 multiply_cosine_fusion
  3.2 1.3 copy.14
  4.5 0.1 convert.10
  4.6 0.2 add_convert_fusion
  4.8 0.1 maximum_bitcast_fusion
  4.9 0.0 copy-start
  4.9 1.0 copy.16.kb
  5.9 0.0 copy-done
  5.9 116.7 %shard_map.102 = (bf16[512,8192]{1,0:T(8,128)(2,1)}, bf16[4,128,2048]{2,1,0:T(8,128)(2,1)}, f32[64,2048]{1,0:T(8,128)}, f32[64,2048]{1,0:T(8,128)}) custom-call(bf16[512,8192]{1,0:T(8,128)(2,1)} %x_hbm.1, bf16[512,512]{1,0:T(8,128)(2,1)} %copy.16.kb, bf16[512,512]{1,0:T(8,128)(2,1)} %bitcast.10, f32[1,8192]{1,0:T(1,128)} %bitcast.13, bf16[64,2048]{1,0:T(8,128)(2,1)} %w.1, ...), custom_call_target="tpu_custom_call" | custom-call | tf_op jit(solution)/shard_map/pallas_call | solution.py:499
  122.6 0.0 copy-start.1
  122.6 0.0 copy-start.3
  122.6 0.0 copy-start.2
  122.6 7.9 %copy.21 = bf16[512,8192]{1,0:T(8,128)(2,1)} copy(bf16[512,8192]{1,0:T(8,128)(2,1)} %get-tuple-element.20) | data formatting | bytes 16777216
  130.5 0.0 copy-done.1
  130.5 1.3 copy.22
  131.8 0.0 copy-done.3
  131.8 0.8 copy.23
  132.6 0.0 copy-done.2
  132.6 0.8 copy.24
  (2 shorter events, 0.0 us)
Async XLA Ops:
  4.9 1.0 copy-start
  122.6 8.0 %copy-start.1 = (bf16[4,128,2048]{2,1,0:T(8,128)(2,1)S(1)}, bf16[4,128,2048]{2,1,0:T(8,128)(2,1)}, u32[]{:S(2)}) copy-start(bf16[4,128,2048]{2,1,0:T(8,128)(2,1)} %get-tuple-element.9) | copy-start | bytes 6291460
  122.6 9.3 %copy-start.3 = (f32[64,2048]{1,0:T(8,128)S(1)}, f32[64,2048]{1,0:T(8,128)}, u32[]{:S(2)}) copy-start(f32[64,2048]{1,0:T(8,128)} %get-tuple-element.22) | copy-start | bytes 1572868
  122.6 10.1 %copy-start.2 = (f32[64,2048]{1,0:T(8,128)S(1)}, f32[64,2048]{1,0:T(8,128)}, u32[]{:S(2)}) copy-start(f32[64,2048]{1,0:T(8,128)} %get-tuple-element.23) | copy-start | bytes 1572868
where the time goes:
time: 134 us; the launch traced here: 133 us
  Pallas kernels  117 us (87%)
  local copies, waits for them, and re-layouts  13.1 us (10%)
  other arithmetic  2.91 us (2%)
    pallas_call x1, Pallas kernels, body(): pl.pallas_call(functools.partial(kernel, ndp, nt, nqx), out_shape=(jax.Sh...  117 us
    unnamed x13, local copies, waits for them, and re-layouts  12.1 us

commit v1 on v0

--- a/solution.py
+++ b/solution.py
@@ -46,9 +46,9 @@
 
 def kernel(
     ndp, nt, nqx, x_hbm, kb, kbt, gain, w, m1, m2,
-    ig_hbm, nw_hbm, nf, ns,
-    x, normed, wf, wg, rcore, r1a, r1b, r2a, r2b, zs, rz, gsum, sinv, cross, nwb, nsend, nrecv,
-    lsem, xsem, osem, a1s, a1r, a2s, a2r, a3s, a3r, b3s, b3r, cs, cr, qs, qr, q2s, q2r,
+    normed, nwb, nf, ns,
+    x, wf, wg, rcore, r1a, r1b, r2a, r2b, zs, rz, gsum, sinv, cross, nsend, nrecv,
+    lsem, xsem, a1s, a1r, a2s, a2r, a3s, a3r, b3s, b3r, cs, cr, qs, qr, q2s, q2r,
     zsd, zr, nss, nsr, ws, wr, vs, vr,
 ):
     nq = ndp // 2
@@ -423,10 +423,7 @@
             n = len(w_second)
             w_second.append(remote(part, part, vs.at[n], vr.at[n], dev_x(k)))
 
-    outs = []
     for k in range(ntile):
-        piece = pl.ds(k * tile, tile)
-
         @pl.loop(0, tile // 16)
         def _(g):
             r = pl.ds(pl.multiple_of(k * tile + g * 16, 16), 16)
@@ -436,22 +433,13 @@
                 s * (normed[r, :].astype(F32) - x[r, :].astype(F32) * s * inner)
             ).astype(BF16)
 
-        copy = pltpu.make_async_copy(normed.at[piece], ig_hbm.at[piece], osem.at[k])
-        copy.start()
-        outs.append(copy)
-
     for copy in w_second:
         copy.wait_recv()
     part = nwb.at[:, pl.ds(nat, rows)]
     last = remote(part, part, vs.at[nb], vr.at[nb], (mate, t))
     last.wait_recv()
-    copy = pltpu.make_async_copy(nwb, nw_hbm, lsem)
-    copy.start()
-    for copy_out in outs:
-        copy_out.wait()
     for sent in sends:
         sent.wait_send()
-    copy.wait()
 
 
 def body(ndp, nt, norm_input, key_grad, positions, norm_gain, key_weight, first_moment, second_moment):
@@ -476,7 +464,6 @@
     nn = 1 + na + nt - 1
     scratch = [
         pltpu.VMEM((tokens, width), BF16),
-        pltpu.VMEM((tokens, width), BF16),
         pltpu.VMEM((nt, features, cols), BF16),
         pltpu.VMEM((nt, features, cols), BF16),
         pltpu.VMEM((nt, nq * rows, cols), BF16),
@@ -489,26 +476,25 @@
         pltpu.VMEM((rows, cols), F32),
         pltpu.VMEM((tokens, 128), F32),
         pltpu.VMEM((tokens, 128), F32),
-        pltpu.VMEM((nq, 2 * rows, cols), BF16),
         pltpu.VMEM((4, 8, 128), F32),
         pltpu.VMEM((nn, 8, 128), F32),
-        dma, dma((ntile,)), dma((ntile,)),
+        dma, dma((ntile,)),
     ]
     for count in (nt - 1, nt * na, nt, nt * nb, nt, nt * nb, nt * na, nt - 1, nn, na, nb + 1):
         scratch += [dma((count,)), dma((count,))]
     input_grad, new_weight, new_first, new_second = pl.pallas_call(
         functools.partial(kernel, ndp, nt, nqx),
         out_shape=(
-            jax.ShapeDtypeStruct((tokens, width), BF16),
-            jax.ShapeDtypeStruct((nq, 2 * rows, cols), BF16),
-            jax.ShapeDtypeStruct((rows, cols), F32),
-            jax.ShapeDtypeStruct((rows, cols), F32),
+            pltpu.VMEM((tokens, width), BF16),
+            pltpu.VMEM((nq, 2 * rows, cols), BF16),
+            pltpu.VMEM((rows, cols), F32),
+            pltpu.VMEM((rows, cols), F32),
         ),
         in_specs=[any_spec] + [vmem] * 6,
-        out_specs=(any_spec, any_spec, vmem, vmem),
+        out_specs=(vmem, vmem, vmem, vmem),
         scratch_shapes=scratch,
         compiler_params=pltpu.CompilerParams(
-            collective_id=0, has_side_effects=True, vmem_limit_bytes=62 * 2**20
+            collective_id=0, has_side_effects=True, vmem_limit_bytes=46 * 2**20
         ),
     )(
         norm_input, back, back.T, norm_gain.astype(F32)[None, :], key_weight, first_moment, second_moment,

time: 134 us -> 128 us (0.955)
  local copies, waits for them, and re-layouts: 13.1 us -> 8.61 us
  Pallas kernels: 117 us -> 115 us
    unnamed x13 -> x7, local copies, waits for them, and re-layouts: 12.1 us -> 7.56 us
    pallas_call x1, Pallas kernels: 117 us -> 115 us  [body(): pl.pallas_call(functools.partial(kernel, ndp, nt, nqx), out_shape=(pltpu....]
where the time goes in v1:
time: 128 us; the launch traced here: 127 us
  Pallas kernels  115 us (90%)
  local copies, waits for them, and re-layouts  8.61 us (7%)
  other arithmetic  2.91 us (2%)
    pallas_call x1, Pallas kernels, body(): pl.pallas_call(functools.partial(kernel, ndp, nt, nqx), out_shape=(pltpu....  115 us
    unnamed x7, local copies, waits for them, and re-layouts  7.56 us

profile of v1, /device:TPU:0, one launch (start us, length us, event | category | flops | bytes accessed | tf_op | source)
XLA Modules:
  0.0 127.1 jit_solution(5229194292292440253)
XLA Ops:
  0.6 0.7 convert_element_type.3
  1.3 1.3 %broadcast_in_dim.11 = f32[8192]{0:T(1024)} convert(bf16[8192]{0:T(1024)(128)(2,1)} %param.10) | non-fusion elementwise | flops 8192 | bytes 49152 | tf_op jit(solution)/shard_map/broadcast_in_dim | solution.py:500
  2.7 0.5 multiply_cosine_fusion
  3.2 1.3 copy.14
  4.5 0.1 convert.10
  4.6 0.2 add_convert_fusion
  4.8 0.1 maximum_bitcast_fusion
  4.9 0.0 copy-start
  4.9 1.0 copy.16.kb
  5.9 0.0 copy-done
  5.9 114.9 %shard_map.102 = (bf16[512,8192]{1,0:T(8,128)(2,1)S(1)}, bf16[4,128,2048]{2,1,0:T(8,128)(2,1)S(1)}, f32[64,2048]{1,0:T(8,128)S(1)}, f32[64,2048]{1,0:T(8,128)S(1)}) custom-call(bf16[512,8192]{1,0:T(8,128)(2,1)} %x_hbm.1, bf16[512,512]{1,0:T(8,128)(2,1)} %copy.16.kb, bf16[512,512]{1,0:T(8,128)(2,1)} %bitcast.11, f32[1,8192]{1,0:T(1,128)} %bitcast.13, ...), custom_call_target="tpu_custom_call" | custom-call | tf_op jit(solution)/shard_map/pallas_call | solution.py:485
  120.8 3.4 %copy.21 = bf16[512,8192]{1,0:T(8,128)(2,1)} copy(bf16[512,8192]{1,0:T(8,128)(2,1)S(1)} %get-tuple-element.16) | data formatting | bytes 16777216
  124.2 1.3 %copy.22 = bf16[512,2048]{1,0:T(8,128)(2,1)} copy(bf16[512,2048]{1,0:T(8,128)(2,1)S(1)} %bitcast.9) | data formatting | bytes 4194304
  125.5 0.8 copy.23
  126.3 0.8 copy.24
  (2 shorter events, 0.0 us)
Async XLA Ops:
  4.9 1.0 copy-start

commit v2 on v1

v2 whole, which is shorter than its diff:
```python
import functools
import math

import jax
import jax.numpy as jnp
import numpy as np
from jax import lax
from jax.experimental import pallas as pl
from jax.experimental.pallas import tpu as pltpu
from jax.sharding import PartitionSpec as P

KV_HEADS = 4
HEAD = 128
ROPE_BASE = 500000.0

eps_norm = 1e-05
beta_one = 0.9
beta_two = 0.95
learn_rate = 0.0003
decay_rate = 0.1
eps_adam = 1e-08

MESH = pl.DeviceIdType.MESH
F32 = jnp.float32
BF16 = jnp.bfloat16


def kernel(
    ndp, nt, nqx, x_hbm, kg_hbm, pos_hbm, gain_hbm, freq_hbm, w_hbm, m1_hbm, m2_hbm,
    grad, nwb, nf, ns,
    x, kg, pos, gain_in, freq, m1, m2, gain, kb, kbt, sks, ssq, cross,
    wf, wg, rcore, r1a, r1b, r2a, r2b, zs, rz, gsum, nsend, nrecv,
    isem, xsem, a1s, a1r, zfs, zfr, b3s, b3r, a3s, a3r, cs, cr, qs, qr, q2s, q2r,
    zsd, zr, nss, nsr, ws, wr, vs, vr,
):
    nq = ndp // 2
    nqy = nq // nqx
    rows, cols = w_hbm.shape
    half = nq * rows
    tokens, width = x.shape
    tile = min(128, tokens)
    ntile = tokens // tile
    hc = cols // 2
    cc = min(512, hc)
    hcol = (pl.ds(0, hc), pl.ds(hc, hc))
    dp = lax.axis_index("dp")
    t = lax.axis_index("tensor")
    c = dp % 2
    q = dp // 2
    qy = q // nqx
    qx = q % nqx
    mate = q * 2 + (1 - c)
    mine = pl.multiple_of(c * half, half)
    theirs = pl.multiple_of((1 - c) * half, half)
    sends = []

    def describe(src, dst, ssem, rsem, dev):
        return pltpu.make_async_remote_copy(
            src_ref=src, dst_ref=dst, send_sem=ssem, recv_sem=rsem, device_id=dev, device_id_type=MESH
        )

    def remote(src, dst, ssem, rsem, dev):
        copy = describe(src, dst, ssem, rsem, dev)
        copy.start()
        sends.append((None, copy))
        return copy

    def pos_x(k):
        return (qx + k) % nqx

    def pos_y(k):
        return (qy + k) % nqy

    def dev_x(k):
        return ((qy * nqx + pos_x(k)) * 2 + c, t)

    def dev_y(k):
        return ((pos_y(k) * nqx + qx) * 2 + c, t)

    def slot(yy, xx):
        return pl.ds(pl.multiple_of(mine + (yy * nqx + xx) * rows, rows), rows)

    def band(yy):
        return pl.ds(pl.multiple_of(mine + yy * nqx * rows, nqx * rows), nqx * rows)

    my_rows = slot(qy, qx)
    steps = sorted(range(1, nt), key=lambda o: (-min(o, nt - o), o)) + [0]

    def dest(i):
        return (t + steps[i]) % nt

    near = jnp.minimum(t, nt - 1 - t)
    low = t < nt - 1 - t

    def block(i):
        if i == 0:
            return t
        d = (i + 1) // 2
        both = t - d if i % 2 else t + d
        return jnp.where(i <= 2 * near, both, jnp.where(low, i, nt - 1 - i))

    def local(src, dst, sem):
        copy = pltpu.make_async_copy(src, dst, sem)
        copy.start()
        return copy

    own = local(w_hbm, wf.at[t, my_rows], isem.at[0])
    kg_in = local(kg_hbm, kg, isem.at[1])
    pos_in = local(pos_hbm, pos, isem.at[2])
    freq_in = local(freq_hbm, freq, isem.at[3])
    x_in = []
    for k in range(ntile):
        piece = pl.ds(k * tile, tile)
        x_in.append(local(x_hbm.at[piece], x.at[piece], xsem.at[k]))
    gain_copy = local(gain_hbm, gain_in, isem.at[4])
    m1_in = local(m1_hbm, m1, isem.at[5])
    m2_in = local(m2_hbm, m2, isem.at[6])

    barrier = pltpu.get_barrier_semaphore()
    for k in range(1, ndp):
        pl.semaphore_signal(barrier, inc=1, device_id=((dp + k) % ndp, t), device_id_type=MESH)
    for k in range(1, nt):
        pl.semaphore_signal(barrier, inc=1, device_id=(dp, (t + k) % nt), device_id_type=MESH)
    pl.semaphore_wait(barrier, ndp - 1 + nt - 1)

    na = nqx + nqy - 2
    first = [
        remote(w_hbm.at[:, hcol[0]], wf.at[t, my_rows, hcol[0]], a1s.at[k - 1], a1r.at[k - 1], dev_x(k))
        for k in range(1, nqx)
    ]
    first += [
        remote(
            w_hbm.at[:, hcol[1]], wf.at[t, my_rows, hcol[1]],
            a1s.at[nqx + k - 2], a1r.at[nqx + k - 2], dev_y(k),
        )
        for k in range(1, nqy)
    ]

    def line_pieces(b, side, dev):
        parts = [wf.at[b, band(qy), hcol[0]]]
        parts += [wf.at[b, slot(yy, qx), hcol[1]] for yy in range(nqy)]
        return [
            describe(part, part, zfs.at[side, b, n], zfr.at[b, n], dev) for n, part in enumerate(parts)
        ]

    def pass_on(b, side):
        to, there = (t + 1, t + 1 < nt) if side == 0 else (t - 1, t >= 1)

        @pl.when(there)
        def _():
            for copy in line_pieces(b, side, (dp, to)):
                copy.start()

    line_sent = []

    def relay(d):
        for side, b, here in ((0, t - d, t - d >= 0), (1, t + d, t + d < nt)):
            @pl.when(here)
            def _(side=side, b=b):
                for copy in line_pieces(b, side, (dp, t)):
                    copy.wait_recv()
                pass_on(b, side)

            line_sent.append((side, b, here))

    nb = (nqy - 1) + (nqx - 1) * nqy
    spread_copies = {}

    def spread(i):
        b = block(i)
        batch = []
        for k in range(1, nqy):
            part = wf.at[b, band(qy), hcol[0]]
            batch.append(remote(part, part, b3s.at[i, k - 1], b3r.at[i, k - 1], dev_y(k)))
        for k in range(1, nqx):
            for yy in range(nqy):
                n = nqy - 1 + (k - 1) * nqy + yy
                part = wf.at[b, slot(yy, qx), hcol[1]]
                batch.append(remote(part, part, b3s.at[i, n], b3r.at[i, n], dev_x(k)))
        spread_copies[i] = batch

    third = {}

    def gather_third(i):
        for copy in spread_copies[i]:
            copy.wait_recv()
        part = wf.at[block(i), pl.ds(mine, half)]
        third[i] = remote(part, part, a3s.at[i], a3r.at[i], (mate, t))

    cross[...] = jnp.zeros_like(cross)
    kg_in.wait()
    pos_in.wait()
    freq_in.wait()
    hh = HEAD // 2
    for k in range(ntile):
        lanes = pl.ds(k * tile, tile)
        angle = freq[:, :tile] * pos[k : k + 1, :tile].astype(F32)
        cosine = jnp.cos(angle)
        sine = jnp.sin(angle)
        turned = kg[pl.ds(k * tile, tile), :].astype(F32).T
        for h in range(KV_HEADS):
            a = turned[h * HEAD : h * HEAD + hh]
            b = turned[h * HEAD + hh : (h + 1) * HEAD]
            for p, value in enumerate((a * cosine + b * sine, b * cosine - a * sine)):
                value = value.astype(BF16)
                for m in range(hh // rows):
                    n = (h * HEAD + p * hh) // rows + m
                    kbt[pl.ds((n % 2) * half + (n // 2) * rows, rows), lanes] = value[
                        m * rows : (m + 1) * rows
                    ]

    def sum_squares(k):
        x_in[k].wait()

        @pl.loop(0, tile // 16)
        def _(g):
            r = pl.ds(pl.multiple_of(k * tile + g * 16, 16), 16)
            total = None
            for b in range(width // 512):
                v = x[r, b * 512 : (b + 1) * 512].astype(F32)
                v = v * v
                v = (v[:, :128] + v[:, 128:256]) + (v[:, 256:384] + v[:, 384:])
                total = v if total is None else total + v
            ssq[r, :] = total

        lanes = pl.ds(k * tile, tile)
        mean = jnp.sum(ssq[lanes, :].T, axis=0, keepdims=True) / width
        sks[:, lanes] = (kbt[:, lanes].astype(F32) * lax.rsqrt(mean + eps_norm)).astype(BF16)

    for k in range(ntile):
        sum_squares(k)
        if k == ntile // 2:
            own.wait()
            for copy in first:
                copy.wait_recv()
            pass_on(t, 0)
            pass_on(t, 1)
            spread(0)

    gain_copy.wait()
    for k in range(width // 128):
        gain[:, k * 128 : (k + 1) * 128] = gain_in[k : k + 1, :].astype(F32)

    core_copies = {}

    def product(i, h):
        j = dest(i)

        @pl.loop(0, hc // cc)
        def _(n):
            off = pl.ds(pl.multiple_of(h * hc + n * cc, cc), cc)
            col = pl.ds(pl.multiple_of(j * cols + h * hc + n * cc, cc), cc)
            total = jnp.dot(sks[...], x[:, col], preferred_element_type=F32)
            wg[j, :, off] = (total * gain[:, col]).astype(BF16)

        n = i * 2 + h
        core_copies[n] = remote(
            wg.at[j, pl.ds(theirs, half), hcol[h]], rcore.at[j, :, hcol[h]], cs.at[n], cr.at[n], (mate, t)
        )

    def pair_sum(i, h):
        j = dest(i)
        core_copies[i * 2 + h].wait_recv()

        @pl.loop(0, half // 16)
        def _(g):
            r = pl.ds(pl.multiple_of(mine + g * 16, 16), 16)
            l = pl.ds(pl.multiple_of(g * 16, 16), 16)
            a = wg[j, r, hcol[h]].astype(F32) + rcore[j, l, hcol[h]].astype(F32)
            wg[j, r, hcol[h]] = a.astype(BF16)

    nx1 = (nqx - 1) * nqy
    q_copies = {}
    q2_copies = {}

    def reduce_first(i, h):
        j = dest(i)
        batch = []
        if h == 0:
            for k in range(1, nqx):
                for yy in range(nqy):
                    n = (k - 1) * nqy + yy
                    src = wg.at[j, slot(yy, pos_x(k)), hcol[0]]
                    batch.append(remote(src, r1a.at[i, n], qs.at[i, n], qr.at[i, n], dev_x(k)))
        else:
            for k in range(1, nqy):
                n = nx1 + k - 1
                src = wg.at[j, band(pos_y(k)), hcol[1]]
                batch.append(remote(src, r1b.at[i, k - 1], qs.at[i, n], qr.at[i, n], dev_y(k)))
        q_copies[i, h] = batch

    def middle(i, h):
        j = dest(i)
        for copy in q_copies[i, h]:
            copy.wait_recv()
        batch = []
        if h == 0:
            @pl.loop(0, rows // 16)
            def _(g):
                l = pl.ds(pl.multiple_of(g * 16, 16), 16)
                for yy in range(nqy):
                    r = pl.ds(pl.multiple_of(mine + (yy * nqx + qx) * rows + g * 16, 16), 16)
                    a = wg[j, r, hcol[0]].astype(F32)
                    for k in range(nqx - 1):
                        a = a + r1a[i, k * nqy + yy, l, :].astype(F32)
                    wg[j, r, hcol[0]] = a.astype(BF16)

            for k in range(1, nqy):
                n = k - 1
                src = wg.at[j, slot(pos_y(k), qx), hcol[0]]
                batch.append(remote(src, r2a.at[i, k - 1], q2s.at[i, n], q2r.at[i, n], dev_y(k)))
        else:
            @pl.loop(0, nqx * rows // 16)
            def _(g):
                l = pl.ds(pl.multiple_of(g * 16, 16), 16)
                r = pl.ds(pl.multiple_of(mine + qy * nqx * rows + g * 16, 16), 16)
                a = wg[j, r, hcol[1]].astype(F32)
                for k in range(nqy - 1):
                    a = a + r1b[i, k, l, :].astype(F32)
                wg[j, r, hcol[1]] = a.astype(BF16)

            for k in range(1, nqx):
                n = nqy - 1 + k - 1
                src = wg.at[j, slot(qy, pos_x(k)), hcol[1]]
                batch.append(remote(src, r2b.at[i, k - 1], q2s.at[i, n], q2r.at[i, n], dev_x(k)))
        q2_copies[i, h] = batch

    z_copies = []

    def final(i):
        j = dest(i)
        for h in range(2):
            for copy in q2_copies[i, h]:
                copy.wait_recv()

        @pl.loop(0, rows // 16)
        def _(g):
            r = pl.ds(pl.multiple_of(g * 16, 16), 16)
            m = pl.ds(pl.multiple_of(mine + q * rows + g * 16, 16), 16)
            for part, other, count in ((hcol[0], r2a, nqy - 1), (hcol[1], r2b, nqx - 1)):
                a = wg[j, m, part].astype(F32)
                for k in range(count):
                    a = a + other[i, k, r, :].astype(F32)
                if i < nt - 1:
                    zs[i, r, part] = a.astype(BF16)
                else:
                    gsum[r, part] = a

        if i < nt - 1:
            z_copies.append(remote(zs.at[i], rz.at[i], zsd.at[i], zr.at[i], (dp, j)))

    uc = min(256, cols)

    def upstream(i):
        b = block(i)
        third[i].wait_recv()

        @pl.loop(0, cols // uc)
        def _(h):
            off = pl.ds(pl.multiple_of(h * uc, uc), uc)
            col = pl.ds(pl.multiple_of(b * cols + h * uc, uc), uc)
            u = jnp.dot(kb[...], wf[b, :, off], preferred_element_type=F32) * gain[:, col]
            grad[:, col] = u.astype(BF16)
            p = u * x[:, col].astype(F32)
            total = p[:, :128]
            for n in range(1, uc // 128):
                total = total + p[:, n * 128 : (n + 1) * 128]
            cross[...] += total

    def turn_back():
        for k in range(ntile):
            lanes = pl.ds(k * tile, tile)
            kb[lanes, :] = kbt[:, lanes].astype(F32).T.astype(BF16)

    units = [(i, h) for i in range(nt) for h in range(2)]
    for n, unit in enumerate(units):
        product(*unit)
        if n > 0:
            pair_sum(*units[n - 1])
            if units[n - 1][0] < 2:
                reduce_first(*units[n - 1])
    pair_sum(*units[-1])
    turn_back()
    gather_third(0)
    for i in range(nt):
        for h in range(2):
            middle(i, h)
            if i + 2 < nt:
                reduce_first(i + 2, h)
        if i == 0:
            relay(1)
            upstream(0)
        if 0 < i < nt - 1:
            relay(i + 1)
        if i > 0:
            final(i - 1)
    for i in range(1, nt):
        spread(i)
    final(nt - 1)
    for copy in z_copies:
        copy.wait_recv()

    nsend[0] = jnp.zeros((8, 128), F32)

    @pl.loop(0, rows // 16)
    def _(g):
        r = pl.ds(pl.multiple_of(g * 16, 16), 16)
        a = gsum[r, :]
        for i in range(nt - 1):
            a = a + rz[i, r, :].astype(F32)
        gsum[r, :] = a
        a = a * a
        a = a[:8] + a[8:]
        total = a[:, :128]
        for k in range(1, cols // 128):
            total = total + a[:, k * 128 : (k + 1) * 128]
        nsend[0] += total

    v = nsend[0]
    base = 0
    groups = (
        [((dp + k) % ndp, t) for k in range(1, ndp)],
        [(dp, (t + k) % nt) for k in range(1, nt)],
    )
    for step, devs in enumerate(groups):
        if step > 0:
            nsend[step] = v
        batch = [
            remote(nsend.at[step], nrecv.at[base + n], nss.at[base + n], nsr.at[base + n], dev)
            for n, dev in enumerate(devs)
        ]
        if step == 0:
            gather_third(1)
        for n, copy in enumerate(batch):
            copy.wait_recv()
            v = v + nrecv[base + n]
        base += len(devs)
    total_square = jnp.sum(jnp.sum(v, axis=1, keepdims=True), axis=0, keepdims=True)
    limit = math.sqrt(kbt.shape[0] * width)
    clip = jnp.minimum(1.0, limit / (jnp.sqrt(total_square) + 1e-06))
    nat = pl.multiple_of(c * rows, rows)
    m1_in.wait()
    m2_in.wait()

    @pl.loop(0, rows // 16)
    def _(g):
        r = pl.ds(pl.multiple_of(g * 16, 16), 16)
        wr_ = pl.ds(pl.multiple_of(mine + q * rows + g * 16, 16), 16)
        clipped = gsum[r, :] * clip
        new_first = beta_one * m1[r, :] + (1.0 - beta_one) * clipped
        new_second = beta_two * m2[r, :] + (1.0 - beta_two) * clipped * clipped
        nf[r, :] = new_first
        ns[r, :] = new_second
        nwb[q, pl.ds(pl.multiple_of(nat + g * 16, 16), 16), :] = (
            wf[t, wr_, :].astype(F32) * (1.0 - learn_rate * decay_rate)
            - learn_rate * new_first / (jnp.sqrt(new_second) + eps_adam)
        ).astype(BF16)

    def piece_of(yy, xx, part):
        return nwb.at[yy * nqx + xx, pl.ds(nat, rows), part]

    w_first = []
    for k in range(1, nqx):
        part = piece_of(qy, qx, hcol[0])
        w_first.append(remote(part, part, ws.at[k - 1], wr.at[k - 1], dev_x(k)))
    for k in range(1, nqy):
        n = nqx - 1 + k - 1
        part = piece_of(qy, qx, hcol[1])
        w_first.append(remote(part, part, ws.at[n], wr.at[n], dev_y(k)))

    for i in range(1, nt - 1):
        upstream(i)
        gather_third(i + 1)

    for copy in w_first:
        copy.wait_recv()
    w_second = []
    for k in range(1, nqy):
        for xx in range(nqx):
            part = piece_of(qy, xx, hcol[0])
            n = len(w_second)
            w_second.append(remote(part, part, vs.at[n], vr.at[n], dev_y(k)))
    for k in range(1, nqx):
        for yy in range(nqy):
            part = piece_of(yy, qx, hcol[1])
            n = len(w_second)
            w_second.append(remote(part, part, vs.at[n], vr.at[n], dev_x(k)))
    upstream(nt - 1)

    sc = min(1024, width)

    @pl.loop(0, tokens // 16)
    def _(g):
        r = pl.ds(pl.multiple_of(g * 16, 16), 16)
        s = lax.rsqrt(jnp.sum(ssq[r, :], axis=1, keepdims=True) / width + eps_norm)
        inner = s * (jnp.sum(cross[r, :], axis=1, keepdims=True) / width)
        up = jnp.broadcast_to(s, (16, sc))
        down = jnp.broadcast_to(s * s * inner, (16, sc))
        for b in range(width // sc):
            col = slice(b * sc, (b + 1) * sc)
            grad[r, col] = (up * grad[r, col].astype(F32) - down * x[r, col].astype(F32)).astype(BF16)

    for copy in w_second:
        copy.wait_recv()
    part = nwb.at[:, pl.ds(nat, rows)]
    n = len(w_second)
    last = remote(part, part, vs.at[n], vr.at[n], (mate, t))
    last.wait_recv()
    for _, sent in sends:
        sent.wait_send()
    for side, b, here in [(0, t, t >= 0), (1, t, t >= 0)] + line_sent:
        there = t + 1 < nt if side == 0 else t >= 1

        @pl.when(jnp.logical_and(here, there))
        def _(side=side, b=b):
            for copy in line_pieces(b, side, (dp, t)):
                copy.wait_send()


def body(ndp, nt, norm_input, key_grad, positions, norm_gain, key_weight, first_moment, second_moment):
    rows, cols = key_weight.shape
    tokens, width = norm_input.shape
    nq = ndp // 2
    features = ndp * rows
    tile = min(128, tokens)
    ntile = tokens // tile
    hh = HEAD // 2
    frequency = ROPE_BASE ** (-(2.0 * np.arange(hh)) / HEAD)
    frequency = np.broadcast_to(frequency.astype(np.float32)[:, None], (hh, 128))
    any_spec = pl.BlockSpec(memory_space=pl.ANY)
    vmem = pl.BlockSpec(memory_space=pltpu.VMEM)
    dma = pltpu.SemaphoreType.DMA
    nqx = math.isqrt(nq)
    while nq % nqx:
        nqx -= 1
    nqy = nq // nqx
    hc = cols // 2
    na = nqx + nqy - 2
    nx1 = (nqx - 1) * nqy
    nw2 = nx1 + (nqy - 1) * nqx
    nn = ndp - 1 + nt - 1
    scratch = [
        pltpu.VMEM((tokens, width), BF16),
        pltpu.VMEM((tokens, features), BF16),
        pltpu.VMEM((ntile, tile), jnp.int32),
        pltpu.VMEM((width // 128, 128), BF16),
        pltpu.VMEM((hh, 128), F32),
        pltpu.VMEM((rows, cols), F32),
        pltpu.VMEM((rows, cols), F32),
        pltpu.VMEM((1, width), F32),
        pltpu.VMEM((tokens, features), BF16),
        pltpu.VMEM((features, tokens), BF16),
        pltpu.VMEM((features, tokens), BF16),
        pltpu.VMEM((tokens, 128), F32),
        pltpu.VMEM((tokens, 128), F32),
        pltpu.VMEM((nt, features, cols), BF16),
        pltpu.VMEM((nt, features, cols), BF16),
        pltpu.VMEM((nt, nq * rows, cols), BF16),
        pltpu.VMEM((nt, nx1, rows, hc), BF16),
        pltpu.VMEM((nt, nqy - 1, nqx * rows, hc), BF16),
        pltpu.VMEM((nt, nqy - 1, rows, hc), BF16),
        pltpu.VMEM((nt, nqx - 1, rows, hc), BF16),
        pltpu.VMEM((nt - 1, rows, cols), BF16),
        pltpu.VMEM((nt - 1, rows, cols), BF16),
        pltpu.VMEM((rows, cols), F32),
        pltpu.VMEM((2, 8, 128), F32),
        pltpu.VMEM((nn, 8, 128), F32),
        dma((7,)), dma((ntile,)),
        dma((na,)), dma((na,)),
        dma((2, nt, 1 + nqy)), dma((nt, 1 + nqy)),
        dma((nt, nqy - 1 + nx1)), dma((nt, nqy - 1 + nx1)),
        dma((nt,)), dma((nt,)),
        dma((2 * nt,)), dma((2 * nt,)),
        dma((nt, nx1 + nqy - 1)), dma((nt, nx1 + nqy - 1)),
        dma((nt, na)), dma((nt, na)),
        dma((nt - 1,)), dma((nt - 1,)),
        dma((nn,)), dma((nn,)),
        dma((na,)), dma((na,)),
        dma((nw2 + 1,)), dma((nw2 + 1,)),
    ]
    input_grad, new_weight, new_first, new_second = pl.pallas_call(
        functools.partial(kernel, ndp, nt, nqx),
        out_shape=(
            pltpu.VMEM((tokens, width), BF16),
            pltpu.VMEM((nq, 2 * rows, cols), BF16),
            pltpu.VMEM((rows, cols), F32),
            pltpu.VMEM((rows, cols), F32),
        ),
        in_specs=[any_spec] * 8,
        out_specs=(vmem, vmem, vmem, vmem),
        scratch_shapes=scratch,
        compiler_params=pltpu.CompilerParams(
            collective_id=0, has_side_effects=True, vmem_limit_bytes=48 * 2**20
        ),
    )(
        norm_input, key_grad, positions.reshape(ntile, tile), norm_gain.reshape(width // 128, 128),
        jnp.asarray(frequency), key_weight, first_moment, second_moment,
    )
    return (input_grad, new_weight.reshape(features, cols), new_first, new_second)


def solution(mesh):
    in_specs = (
        P(("dp", "tensor"), None),
        P(("dp", "tensor"), None),
        P(("dp", "tensor")),
        P(),
        P("dp", "tensor"),
        P("dp", "tensor"),
        P("dp", "tensor"),
    )
    out_specs = (P(("dp", "tensor"), None), P(None, "tensor"), P("dp", "tensor"), P("dp", "tensor"))
    return jax.shard_map(
        functools.partial(body, mesh.shape["dp"], mesh.shape["tensor"]),
        mesh=mesh, in_specs=in_specs, out_specs=out_specs, check_vma=False,
    )
```

time: 128 us -> 110 us (0.86)
  Pallas kernels: 115 us -> 101 us
  other arithmetic: 2.91 us -> 0 us
    pallas_call x1, Pallas kernels: 115 us -> 101 us  [body(): pl.pallas_call(functools.partial(kernel, ndp, nt, nqx), out_shape=(pltpu....]
    another operation x0 -> x1, local copies, waits for them, and re-layouts: none -> 1.35 us
    broadcast_in_dim x1 -> x0, other arithmetic: 1.33 us -> none  [body(): norm_gain.astype(F32)[None, :]]
    unnamed x7 -> x4, local copies, waits for them, and re-layouts: 7.56 us -> 6.3 us
where the time goes in v2:
time: 110 us
  Pallas kernels  101 us (92%)
  local copies, waits for them, and re-layouts  7.65 us (7%)
    pallas_call x1, Pallas kernels, body(): pl.pallas_call(functools.partial(kernel, ndp, nt, nqx), out_shape=(pltpu....  101 us
    unnamed x4, local copies, waits for them, and re-layouts  6.3 us

profile of v2, /device:TPU:0, one launch (start us, length us, event | category | flops | bytes accessed | tf_op | source)
XLA Modules:
  0.0 109.6 jit_solution(4846995387749094716)
XLA Ops:
  0.6 1.3 %jit_solution_.3.freq_hbm = f32[64,128]{1,0:T(8,128)} broadcast(f32[64]{0:T(128)} %constant.2.clone), dimensions={0} | broadcast | bytes 33024 | tf_op jit(solution)
  2.0 101.3 %shard_map.111 = (bf16[512,8192]{1,0:T(8,128)(2,1)S(1)}, bf16[4,128,2048]{2,1,0:T(8,128)(2,1)S(1)}, f32[64,2048]{1,0:T(8,128)S(1)}, f32[64,2048]{1,0:T(8,128)S(1)}) custom-call(bf16[512,8192]{1,0:T(8,128)(2,1)} %x_hbm.1, bf16[512,512]{1,0:T(8,128)(2,1)} %kg_hbm.1, s32[4,128]{1,0:T(4,128)} %bitcast.5, bf16[64,128]{1,0:T(8,128)(2,1)} %bitcast.4, ...), custom_call_target="tpu_custom_call" | custom-call | tf_op jit(solution)/shard_map/pallas_call | solution.py:581
  103.3 3.4 %copy.16 = bf16[512,8192]{1,0:T(8,128)(2,1)} copy(bf16[512,8192]{1,0:T(8,128)(2,1)S(1)} %get-tuple-element.12) | data formatting | bytes 16777216
  106.7 1.3 %copy.17 = bf16[512,2048]{1,0:T(8,128)(2,1)} copy(bf16[512,2048]{1,0:T(8,128)(2,1)S(1)} %bitcast.3) | data formatting | bytes 4194304
  108.0 0.8 copy.18
  108.8 0.8 copy.19

commit v3 on v2

--- a/solution.py
+++ b/solution.py
@@ -31,7 +31,7 @@
     x, kg, pos, gain_in, freq, m1, m2, gain, kb, kbt, sks, ssq, cross,
     wf, wg, rcore, r1a, r1b, r2a, r2b, zs, rz, gsum, nsend, nrecv,
     isem, xsem, a1s, a1r, zfs, zfr, b3s, b3r, a3s, a3r, cs, cr, qs, qr, q2s, q2r,
-    zsd, zr, nss, nsr, ws, wr, vs, vr,
+    zsd, zr, nss, nsr, ws, wr, vs, vr, us, ur,
 ):
     nq = ndp // 2
     nqy = nq // nqx
@@ -121,80 +121,15 @@
         pl.semaphore_signal(barrier, inc=1, device_id=((dp + k) % ndp, t), device_id_type=MESH)
     for k in range(1, nt):
         pl.semaphore_signal(barrier, inc=1, device_id=(dp, (t + k) % nt), device_id_type=MESH)
-    pl.semaphore_wait(barrier, ndp - 1 + nt - 1)
-
-    na = nqx + nqy - 2
-    first = [
-        remote(w_hbm.at[:, hcol[0]], wf.at[t, my_rows, hcol[0]], a1s.at[k - 1], a1r.at[k - 1], dev_x(k))
-        for k in range(1, nqx)
-    ]
-    first += [
-        remote(
-            w_hbm.at[:, hcol[1]], wf.at[t, my_rows, hcol[1]],
-            a1s.at[nqx + k - 2], a1r.at[nqx + k - 2], dev_y(k),
-        )
-        for k in range(1, nqy)
-    ]
-
-    def line_pieces(b, side, dev):
-        parts = [wf.at[b, band(qy), hcol[0]]]
-        parts += [wf.at[b, slot(yy, qx), hcol[1]] for yy in range(nqy)]
-        return [
-            describe(part, part, zfs.at[side, b, n], zfr.at[b, n], dev) for n, part in enumerate(parts)
-        ]
-
-    def pass_on(b, side):
-        to, there = (t + 1, t + 1 < nt) if side == 0 else (t - 1, t >= 1)
-
-        @pl.when(there)
-        def _():
-            for copy in line_pieces(b, side, (dp, to)):
-                copy.start()
-
-    line_sent = []
-
-    def relay(d):
-        for side, b, here in ((0, t - d, t - d >= 0), (1, t + d, t + d < nt)):
-            @pl.when(here)
-            def _(side=side, b=b):
-                for copy in line_pieces(b, side, (dp, t)):
-                    copy.wait_recv()
-                pass_on(b, side)
-
-            line_sent.append((side, b, here))
-
-    nb = (nqy - 1) + (nqx - 1) * nqy
-    spread_copies = {}
-
-    def spread(i):
-        b = block(i)
-        batch = []
-        for k in range(1, nqy):
-            part = wf.at[b, band(qy), hcol[0]]
-            batch.append(remote(part, part, b3s.at[i, k - 1], b3r.at[i, k - 1], dev_y(k)))
-        for k in range(1, nqx):
-            for yy in range(nqy):
-                n = nqy - 1 + (k - 1) * nqy + yy
-                part = wf.at[b, slot(yy, qx), hcol[1]]
-                batch.append(remote(part, part, b3s.at[i, n], b3r.at[i, n], dev_x(k)))
-        spread_copies[i] = batch
-
-    third = {}
-
-    def gather_third(i):
-        for copy in spread_copies[i]:
-            copy.wait_recv()
-        part = wf.at[block(i), pl.ds(mine, half)]
-        third[i] = remote(part, part, a3s.at[i], a3r.at[i], (mate, t))
-
     cross[...] = jnp.zeros_like(cross)
     kg_in.wait()
     pos_in.wait()
     freq_in.wait()
     hh = HEAD // 2
+    turn = jnp.broadcast_to(freq[...], (128, 128)).T[:hh, :tile]
     for k in range(ntile):
         lanes = pl.ds(k * tile, tile)
-        angle = freq[:, :tile] * pos[k : k + 1, :tile].astype(F32)
+        angle = turn * pos[k : k + 1, :].astype(F32)
         cosine = jnp.cos(angle)
         sine = jnp.sin(angle)
         turned = kg[pl.ds(k * tile, tile), :].astype(F32).T
@@ -209,6 +144,85 @@
                         m * rows : (m + 1) * rows
                     ]
 
+    pl.semaphore_wait(barrier, ndp - 1 + nt - 1)
+
+    na = nqx + nqy - 2
+    first = [
+        remote(w_hbm.at[:, hcol[0]], wf.at[t, my_rows, hcol[0]], a1s.at[k - 1], a1r.at[k - 1], dev_x(k))
+        for k in range(1, nqx)
+    ]
+    first += [
+        remote(
+            w_hbm.at[:, hcol[1]], wf.at[t, my_rows, hcol[1]],
+            a1s.at[nqx + k - 2], a1r.at[nqx + k - 2], dev_y(k),
+        )
+        for k in range(1, nqy)
+    ]
+
+    nb = nqx * (nqy - 1) + (nqx - 1) * nqy
+    spread_copies = {}
+
+    def spread(i, near=(False, True)):
+        b = block(i)
+        batch = spread_copies.setdefault(i, [])
+        n = 0
+        for h, count, other, dev in ((0, nqx, nqy, dev_y), (1, nqy, nqx, dev_x)):
+            for k in range(1, other):
+                for m in range(count):
+                    place = slot(qy, pos_x(m)) if h == 0 else slot(pos_y(m), qx)
+                    if (m == 0) in near:
+                        part = wf.at[b, place, hcol[h]]
+                        src = w_hbm.at[:, hcol[h]] if i == 0 and m == 0 else part
+                        batch.append(remote(src, part, b3s.at[i, n], b3r.at[i, n], dev(k)))
+                    n += 1
+
+    spread(0, (True,))
+
+    def line_pieces(b, side, p, dev):
+        if p == 0:
+            parts = [wf.at[b, my_rows]]
+        else:
+            parts = [wf.at[b, slot(qy, pos_x(k)), hcol[0]] for k in range(1, nqx)]
+            parts += [wf.at[b, slot(pos_y(k), qx), hcol[1]] for k in range(1, nqy)]
+        return [
+            describe(part, part, zfs.at[side, b, p + n], zfr.at[b, p + n], dev)
+            for n, part in enumerate(parts)
+        ]
+
+    def pass_on(b, side, p):
+        to, there = (t + 1, t + 1 < nt) if side == 0 else (t - 1, t >= 1)
+
+        @pl.when(there)
+        def _():
+            for copy in line_pieces(b, side, p, (dp, to)):
+                copy.start()
+
+    line_sent = [(0, t, t >= 0), (1, t, t >= 0)]
+
+    def relay(d, p):
+        for side, b, here in ((0, t - d, t - d >= 0), (1, t + d, t + d < nt)):
+            @pl.when(here)
+            def _(side=side, b=b):
+                for copy in line_pieces(b, side, p, (dp, t)):
+                    copy.wait_recv()
+                pass_on(b, side, p)
+
+            if p == 0:
+                line_sent.append((side, b, here))
+
+    for side, to, there in ((0, t + 1, t + 1 < nt), (1, t - 1, t >= 1)):
+        @pl.when(there)
+        def _(side=side, to=to):
+            describe(w_hbm, wf.at[t, my_rows], zfs.at[side, t, 0], zfr.at[t, 0], (dp, to)).start()
+
+    third = {}
+
+    def gather_third(i):
+        for copy in spread_copies[i]:
+            copy.wait_recv()
+        part = wf.at[block(i), pl.ds(mine, half)]
+        third[i] = remote(part, part, a3s.at[i], a3r.at[i], (mate, t))
+
     def sum_squares(k):
         x_in[k].wait()
 
@@ -229,13 +243,6 @@
 
     for k in range(ntile):
         sum_squares(k)
-        if k == ntile // 2:
-            own.wait()
-            for copy in first:
-                copy.wait_recv()
-            pass_on(t, 0)
-            pass_on(t, 1)
-            spread(0)
 
     gain_copy.wait()
     for k in range(width // 128):
@@ -360,6 +367,8 @@
             off = pl.ds(pl.multiple_of(h * uc, uc), uc)
             col = pl.ds(pl.multiple_of(b * cols + h * uc, uc), uc)
             u = jnp.dot(kb[...], wf[b, :, off], preferred_element_type=F32) * gain[:, col]
+            scale = ssq[...]
+            u = jnp.concatenate([u[:, n * 128 : (n + 1) * 128] * scale for n in range(uc // 128)], axis=1)
             grad[:, col] = u.astype(BF16)
             p = u * x[:, col].astype(F32)
             total = p[:, :128]
@@ -371,31 +380,50 @@
         for k in range(ntile):
             lanes = pl.ds(k * tile, tile)
             kb[lanes, :] = kbt[:, lanes].astype(F32).T.astype(BF16)
+            mean = jnp.sum(ssq[lanes, :], axis=1, keepdims=True) / width
+            ssq[lanes, :] = jnp.broadcast_to(lax.rsqrt(mean + eps_norm), (tile, 128))
 
     units = [(i, h) for i in range(nt) for h in range(2)]
+    early = min(4, len(units))
     for n, unit in enumerate(units):
         product(*unit)
+        if n == 1:
+            own.wait()
+            for copy in first:
+                copy.wait_recv()
+            pass_on(t, 0, 1)
+            pass_on(t, 1, 1)
+        if n == len(units) - 1:
+            relay(1, 1)
         if n > 0:
             pair_sum(*units[n - 1])
-            if units[n - 1][0] < 2:
+            if n <= early:
                 reduce_first(*units[n - 1])
+        if n == early:
+            relay(1, 0)
     pair_sum(*units[-1])
     turn_back()
-    gather_third(0)
-    for i in range(nt):
-        for h in range(2):
-            middle(i, h)
-            if i + 2 < nt:
-                reduce_first(i + 2, h)
-        if i == 0:
-            relay(1)
-            upstream(0)
-        if 0 < i < nt - 1:
-            relay(i + 1)
-        if i > 0:
-            final(i - 1)
-    for i in range(1, nt):
-        spread(i)
+
+    def both_middle(i):
+        middle(i, 0)
+        middle(i, 1)
+        if i + 2 < nt:
+            reduce_first(i + 2, 0)
+            reduce_first(i + 2, 1)
+
+    both_middle(0)
+    both_middle(1)
+    final(0)
+    for i in range(2, nt):
+        both_middle(i)
+        if i == nt - 1:
+            spread(0, (False,))
+            spread(1)
+        final(i - 1)
+        if i > 2:
+            relay(i - 1, 0)
+            if i < nt - 1:
+                relay(i - 1, 1)
     final(nt - 1)
     for copy in z_copies:
         copy.wait_recv()
@@ -430,7 +458,17 @@
             for n, dev in enumerate(devs)
         ]
         if step == 0:
+            if nt > 2:
+                relay(nt - 2, 1)
+            for i in range(2, nt - 1):
+                spread(i)
+            gather_third(0)
+        else:
+            upstream(0)
             gather_third(1)
+            relay(nt - 1, 0)
+            relay(nt - 1, 1)
+            spread(nt - 1)
         for n, copy in enumerate(batch):
             copy.wait_recv()
             v = v + nrecv[base + n]
@@ -469,8 +507,8 @@
         w_first.append(remote(part, part, ws.at[n], wr.at[n], dev_y(k)))
 
     for i in range(1, nt - 1):
+        gather_third(i + 1)
         upstream(i)
-        gather_third(i + 1)
 
     for copy in w_first:
         copy.wait_recv()
@@ -485,36 +523,64 @@
             part = piece_of(yy, qx, hcol[1])
             n = len(w_second)
             w_second.append(remote(part, part, vs.at[n], vr.at[n], dev_x(k)))
+    nw1 = len(w_second)
+    lasts = [
+        remote(part, part, us.at[n], ur.at[n], (mate, t))
+        for n, part in enumerate(
+            [piece_of(qy, pos_x(m), hcol[0]) for m in range(nqx)]
+            + [piece_of(pos_y(m), qx, hcol[1]) for m in range(nqy)]
+        )
+    ]
     upstream(nt - 1)
 
-    sc = min(1024, width)
-
-    @pl.loop(0, tokens // 16)
-    def _(g):
-        r = pl.ds(pl.multiple_of(g * 16, 16), 16)
-        s = lax.rsqrt(jnp.sum(ssq[r, :], axis=1, keepdims=True) / width + eps_norm)
-        inner = s * (jnp.sum(cross[r, :], axis=1, keepdims=True) / width)
-        up = jnp.broadcast_to(s, (16, sc))
-        down = jnp.broadcast_to(s * s * inner, (16, sc))
-        for b in range(width // sc):
-            col = slice(b * sc, (b + 1) * sc)
-            grad[r, col] = (up * grad[r, col].astype(F32) - down * x[r, col].astype(F32)).astype(BF16)
-
+    for k in range(ntile):
+        lanes = pl.ds(k * tile, tile)
+        down = ssq[lanes, :1] * (jnp.sum(cross[lanes, :], axis=1, keepdims=True) / width)
+        cross[lanes, :] = jnp.broadcast_to(down, (tile, 128))
+
+    def finish(a, b):
+        @pl.loop(a // 16, b // 16)
+        def _(g):
+            r = pl.ds(pl.multiple_of(g * 16, 16), 16)
+            down = cross[r, :]
+            for n in range(width // 128):
+                col = slice(n * 128, (n + 1) * 128)
+                grad[r, col] = (grad[r, col].astype(F32) - down * x[r, col].astype(F32)).astype(BF16)
+
+    finish(0, tokens // 2)
     for copy in w_second:
         copy.wait_recv()
-    part = nwb.at[:, pl.ds(nat, rows)]
-    n = len(w_second)
-    last = remote(part, part, vs.at[n], vr.at[n], (mate, t))
-    last.wait_recv()
+    lasts += [
+        remote(part, part, vs.at[nw1 + n], vr.at[nw1 + n], (mate, t))
+        for n, part in enumerate(
+            [piece_of(pos_y(k), pos_x(m), hcol[0]) for k in range(1, nqy) for m in range(nqx)]
+            + [piece_of(pos_y(m), pos_x(k), hcol[1]) for k in range(1, nqx) for m in range(nqy)]
+        )
+    ]
+    finish(tokens // 2, tokens)
+    for copy in lasts:
+        copy.wait_recv()
     for _, sent in sends:
         sent.wait_send()
-    for side, b, here in [(0, t, t >= 0), (1, t, t >= 0)] + line_sent:
+    for side, b, here in line_sent:
         there = t + 1 < nt if side == 0 else t >= 1
 
         @pl.when(jnp.logical_and(here, there))
         def _(side=side, b=b):
-            for copy in line_pieces(b, side, (dp, t)):
-                copy.wait_send()
+            for p in range(2):
+                for copy in line_pieces(b, side, p, (dp, t)):
+                    copy.wait_send()
+
+
+def write_out(a, b, c, d, a_out, b_out, c_out, d_out, sem):
+    copies = [
+        pltpu.make_async_copy(src, dst, sem.at[n])
+        for n, (src, dst) in enumerate(((a, a_out), (b, b_out), (c, c_out), (d, d_out)))
+    ]
+    for copy in copies:
+        copy.start()
+    for copy in copies:
+        copy.wait()
 
 
 def body(ndp, nt, norm_input, key_grad, positions, norm_gain, key_weight, first_moment, second_moment):
@@ -526,7 +592,7 @@
     ntile = tokens // tile
     hh = HEAD // 2
     frequency = ROPE_BASE ** (-(2.0 * np.arange(hh)) / HEAD)
-    frequency = np.broadcast_to(frequency.astype(np.float32)[:, None], (hh, 128))
+    frequency = np.resize(frequency.astype(np.float32), (1, 128))
     any_spec = pl.BlockSpec(memory_space=pl.ANY)
     vmem = pl.BlockSpec(memory_space=pltpu.VMEM)
     dma = pltpu.SemaphoreType.DMA
@@ -544,7 +610,7 @@
         pltpu.VMEM((tokens, features), BF16),
         pltpu.VMEM((ntile, tile), jnp.int32),
         pltpu.VMEM((width // 128, 128), BF16),
-        pltpu.VMEM((hh, 128), F32),
+        pltpu.VMEM((1, 128), F32),
         pltpu.VMEM((rows, cols), F32),
         pltpu.VMEM((rows, cols), F32),
         pltpu.VMEM((1, width), F32),
@@ -567,8 +633,8 @@
         pltpu.VMEM((nn, 8, 128), F32),
         dma((7,)), dma((ntile,)),
         dma((na,)), dma((na,)),
-        dma((2, nt, 1 + nqy)), dma((nt, 1 + nqy)),
-        dma((nt, nqy - 1 + nx1)), dma((nt, nqy - 1 + nx1)),
+        dma((2, nt, 1 + na)), dma((nt, 1 + na)),
+        dma((nt, nw2)), dma((nt, nw2)),
         dma((nt,)), dma((nt,)),
         dma((2 * nt,)), dma((2 * nt,)),
         dma((nt, nx1 + nqy - 1)), dma((nt, nx1 + nqy - 1)),
@@ -576,9 +642,10 @@
         dma((nt - 1,)), dma((nt - 1,)),
         dma((nn,)), dma((nn,)),
         dma((na,)), dma((na,)),
-        dma((nw2 + 1,)), dma((nw2 + 1,)),
+        dma((2 * nw2,)), dma((2 * nw2,)),
+        dma((nqx + nqy,)), dma((nqx + nqy,)),
     ]
-    input_grad, new_weight, new_first, new_second = pl.pallas_call(
+    results = pl.pallas_call(
         functools.partial(kernel, ndp, nt, nqx),
         out_shape=(
             pltpu.VMEM((tokens, width), BF16),
@@ -596,6 +663,15 @@
         norm_input, key_grad, positions.reshape(ntile, tile), norm_gain.reshape(width // 128, 128),
         jnp.asarray(frequency), key_weight, first_moment, second_moment,
     )
+    results = [pltpu.with_memory_space_constraint(r, pltpu.VMEM) for r in results]
+    input_grad, new_weight, new_first, new_second = pl.pallas_call(
+        write_out,
+        out_shape=[jax.ShapeDtypeStruct(r.shape, r.dtype) for r in results],
+        in_specs=[vmem] * 4,
+        out_specs=[any_spec] * 4,
+        scratch_shapes=[dma((4,))],
+        compiler_params=pltpu.CompilerParams(vmem_limit_bytes=2**20),
+    )(*results)
     return (input_grad, new_weight.reshape(features, cols), new_first, new_second)
 
 

time: 110 us -> 88.5 us (0.80)
  Pallas kernels: 101 us -> 87.7 us
  local copies, waits for them, and re-layouts: 7.65 us -> 0 us
    pallas_call x1, Pallas kernels: 101 us -> 83.4 us  [body(): pl.pallas_call(functools.partial(kernel, ndp, nt, nqx), out_shape=(pltpu....]
    unnamed x4 -> x0, local copies, waits for them, and re-layouts: 6.3 us -> none
    pallas_call x0 -> x1, Pallas kernels: none -> 4.38 us  [body(): pl.pallas_call(write_out, out_shape=[jax.ShapeDtypeStruct(r.shape, r.dtyp...]
    another operation x1 -> x0, local copies, waits for them, and re-layouts: 1.35 us -> none
where the time goes in v3:
time: 88.5 us; the launch traced here: 88.4 us
  Pallas kernels  87.7 us (99%)
    pallas_call x1, Pallas kernels, body(): pl.pallas_call(functools.partial(kernel, ndp, nt, nqx), out_shape=(pltpu....  83.4 us
    pallas_call x1, Pallas kernels, body(): pl.pallas_call(write_out, out_shape=[jax.ShapeDtypeStruct(r.shape, r.dtyp...  4.38 us

profile of v3, /device:TPU:0, one launch (start us, length us, event | category | flops | bytes accessed | tf_op | source)
XLA Modules:
  0.0 88.4 jit_solution(2178013753784481101)
XLA Ops:
  0.6 83.4 %shard_map.111 = (bf16[512,8192]{1,0:T(8,128)(2,1)S(1)}, bf16[4,128,2048]{2,1,0:T(8,128)(2,1)S(1)}, f32[64,2048]{1,0:T(8,128)S(1)}, f32[64,2048]{1,0:T(8,128)S(1)}) custom-call(bf16[512,8192]{1,0:T(8,128)(2,1)} %x_hbm.1, bf16[512,512]{1,0:T(8,128)(2,1)} %kg_hbm.1, s32[4,128]{1,0:T(4,128)} %bitcast.4, bf16[64,128]{1,0:T(8,128)(2,1)} %bitcast.3, ...), custom_call_target="tpu_custom_call" | custom-call | tf_op jit(solution)/shard_map/pallas_call | solution.py:648
  84.0 4.4 %shard_map.112 = (bf16[512,8192]{1,0:T(8,128)(2,1)}, bf16[4,128,2048]{2,1,0:T(8,128)(2,1)}, f32[64,2048]{1,0:T(8,128)}, f32[64,2048]{1,0:T(8,128)}) custom-call(bf16[512,8192]{1,0:T(8,128)(2,1)S(1)} %get-tuple-element.12.a, bf16[4,128,2048]{2,1,0:T(8,128)(2,1)S(1)} %get-tuple-element.13.b, f32[64,2048]{1,0:T(8,128)S(1)} %get-tuple-element.14.c, ...), custom_call_target="tpu_custom_call" | custom-call | tf_op jit(solution)/shard_map/pallas_call | solution.py:667

commit v4 on v3

--- a/solution.py
+++ b/solution.py
@@ -27,8 +27,8 @@
 
 def kernel(
     ndp, nt, nqx, x_hbm, kg_hbm, pos_hbm, gain_hbm, freq_hbm, w_hbm, m1_hbm, m2_hbm,
-    grad, nwb, nf, ns,
-    x, kg, pos, gain_in, freq, m1, m2, gain, kb, kbt, sks, ssq, cross,
+    grad, x, cross, nwb, nf, ns,
+    kg, pos, gain_in, freq, m1, m2, gain, kb, kbt, sks, ssq,
     wf, wg, rcore, r1a, r1b, r2a, r2b, zs, rz, gsum, nsend, nrecv,
     isem, xsem, a1s, a1r, zfs, zfr, b3s, b3r, a3s, a3r, cs, cr, qs, qr, q2s, q2r,
     zsd, zr, nss, nsr, ws, wr, vs, vr, us, ur,
@@ -52,7 +52,7 @@
     mate = q * 2 + (1 - c)
     mine = pl.multiple_of(c * half, half)
     theirs = pl.multiple_of((1 - c) * half, half)
-    sends = []
+    sent = []
 
     def describe(src, dst, ssem, rsem, dev):
         return pltpu.make_async_remote_copy(
@@ -60,10 +60,19 @@
         )
 
     def remote(src, dst, ssem, rsem, dev):
-        copy = describe(src, dst, ssem, rsem, dev)
-        copy.start()
-        sends.append((None, copy))
-        return copy
+        describe(src, dst, ssem, rsem, dev).start()
+
+    def arrived(like, rsem):
+        describe(like, like, a1s, rsem, (mate, t)).wait_recv()
+
+    def left(like, ssem):
+        describe(like, like, ssem, a1r, (mate, t)).wait_send()
+
+    def chunks(n):
+        return wg.at[0, pl.ds(0, n * rows), hcol[0]]
+
+    def layers(n):
+        return wg.at[:, pl.ds(0, n * rows), hcol[0]]
 
     def pos_x(k):
         return (qx + k) % nqx
@@ -147,25 +156,17 @@
     pl.semaphore_wait(barrier, ndp - 1 + nt - 1)
 
     na = nqx + nqy - 2
-    first = [
-        remote(w_hbm.at[:, hcol[0]], wf.at[t, my_rows, hcol[0]], a1s.at[k - 1], a1r.at[k - 1], dev_x(k))
-        for k in range(1, nqx)
-    ]
-    first += [
-        remote(
-            w_hbm.at[:, hcol[1]], wf.at[t, my_rows, hcol[1]],
-            a1s.at[nqx + k - 2], a1r.at[nqx + k - 2], dev_y(k),
-        )
-        for k in range(1, nqy)
-    ]
-
-    nb = nqx * (nqy - 1) + (nqx - 1) * nqy
-    spread_copies = {}
+    nx1 = (nqx - 1) * nqy
+    ny1 = (nqy - 1) * nqx
+    nw2 = nx1 + ny1
+    for k in range(1, nqx):
+        remote(w_hbm.at[:, hcol[0]], wf.at[t, my_rows, hcol[0]], a1s, a1r, dev_x(k))
+    for k in range(1, nqy):
+        remote(w_hbm.at[:, hcol[1]], wf.at[t, my_rows, hcol[1]], a1s, a1r, dev_y(k))
+    sent.append((chunks(na), a1s))
 
     def spread(i, near=(False, True)):
         b = block(i)
-        batch = spread_copies.setdefault(i, [])
-        n = 0
         for h, count, other, dev in ((0, nqx, nqy, dev_y), (1, nqy, nqx, dev_x)):
             for k in range(1, other):
                 for m in range(count):
@@ -173,9 +174,9 @@
                     if (m == 0) in near:
                         part = wf.at[b, place, hcol[h]]
                         src = w_hbm.at[:, hcol[h]] if i == 0 and m == 0 else part
-                        batch.append(remote(src, part, b3s.at[i, n], b3r.at[i, n], dev(k)))
-                    n += 1
-
+                        remote(src, part, b3s, b3r.at[i], dev(k))
+
+    sent.append((layers(nw2), b3s))
     spread(0, (True,))
 
     def line_pieces(b, side, p, dev):
@@ -184,10 +185,7 @@
         else:
             parts = [wf.at[b, slot(qy, pos_x(k)), hcol[0]] for k in range(1, nqx)]
             parts += [wf.at[b, slot(pos_y(k), qx), hcol[1]] for k in range(1, nqy)]
-        return [
-            describe(part, part, zfs.at[side, b, p + n], zfr.at[b, p + n], dev)
-            for n, part in enumerate(parts)
-        ]
+        return [describe(part, part, zfs.at[side, b], zfr.at[b, p], dev) for part in parts]
 
     def pass_on(b, side, p):
         to, there = (t + 1, t + 1 < nt) if side == 0 else (t - 1, t >= 1)
@@ -203,8 +201,7 @@
         for side, b, here in ((0, t - d, t - d >= 0), (1, t + d, t + d < nt)):
             @pl.when(here)
             def _(side=side, b=b):
-                for copy in line_pieces(b, side, p, (dp, t)):
-                    copy.wait_recv()
+                arrived(chunks(2 if p == 0 else na), zfr.at[b, p])
                 pass_on(b, side, p)
 
             if p == 0:
@@ -213,15 +210,14 @@
     for side, to, there in ((0, t + 1, t + 1 < nt), (1, t - 1, t >= 1)):
         @pl.when(there)
         def _(side=side, to=to):
-            describe(w_hbm, wf.at[t, my_rows], zfs.at[side, t, 0], zfr.at[t, 0], (dp, to)).start()
-
-    third = {}
+            describe(w_hbm, wf.at[t, my_rows], zfs.at[side, t], zfr.at[t, 0], (dp, to)).start()
 
     def gather_third(i):
-        for copy in spread_copies[i]:
-            copy.wait_recv()
+        arrived(chunks(nw2), b3r.at[i])
         part = wf.at[block(i), pl.ds(mine, half)]
-        third[i] = remote(part, part, a3s.at[i], a3r.at[i], (mate, t))
+        remote(part, part, a3s, a3r.at[i], (mate, t))
+
+    sent.append((wg.at[:, pl.ds(0, half)], a3s))
 
     def sum_squares(k):
         x_in[k].wait()
@@ -248,7 +244,7 @@
     for k in range(width // 128):
         gain[:, k * 128 : (k + 1) * 128] = gain_in[k : k + 1, :].astype(F32)
 
-    core_copies = {}
+    sent.append((wg.at[:, pl.ds(0, half)], cs))
 
     def product(i, h):
         j = dest(i)
@@ -261,13 +257,11 @@
             wg[j, :, off] = (total * gain[:, col]).astype(BF16)
 
         n = i * 2 + h
-        core_copies[n] = remote(
-            wg.at[j, pl.ds(theirs, half), hcol[h]], rcore.at[j, :, hcol[h]], cs.at[n], cr.at[n], (mate, t)
-        )
+        remote(wg.at[j, pl.ds(theirs, half), hcol[h]], rcore.at[j, :, hcol[h]], cs, cr.at[n], (mate, t))
 
     def pair_sum(i, h):
         j = dest(i)
-        core_copies[i * 2 + h].wait_recv()
+        arrived(rcore.at[j, :, hcol[h]], cr.at[i * 2 + h])
 
         @pl.loop(0, half // 16)
         def _(g):
@@ -276,31 +270,25 @@
             a = wg[j, r, hcol[h]].astype(F32) + rcore[j, l, hcol[h]].astype(F32)
             wg[j, r, hcol[h]] = a.astype(BF16)
 
-    nx1 = (nqx - 1) * nqy
-    q_copies = {}
-    q2_copies = {}
-
     def reduce_first(i, h):
         j = dest(i)
-        batch = []
         if h == 0:
             for k in range(1, nqx):
                 for yy in range(nqy):
                     n = (k - 1) * nqy + yy
                     src = wg.at[j, slot(yy, pos_x(k)), hcol[0]]
-                    batch.append(remote(src, r1a.at[i, n], qs.at[i, n], qr.at[i, n], dev_x(k)))
+                    remote(src, r1a.at[i, n], qs, qr.at[i, 0], dev_x(k))
         else:
             for k in range(1, nqy):
-                n = nx1 + k - 1
                 src = wg.at[j, band(pos_y(k)), hcol[1]]
-                batch.append(remote(src, r1b.at[i, k - 1], qs.at[i, n], qr.at[i, n], dev_y(k)))
-        q_copies[i, h] = batch
+                remote(src, r1b.at[i, k - 1], qs, qr.at[i, 1], dev_y(k))
+
+    sent.append((layers(nw2), qs))
+    sent.append((layers(na), q2s))
 
     def middle(i, h):
         j = dest(i)
-        for copy in q_copies[i, h]:
-            copy.wait_recv()
-        batch = []
+        arrived(chunks(ny1 if h else nx1), qr.at[i, h])
         if h == 0:
             @pl.loop(0, rows // 16)
             def _(g):
@@ -313,9 +301,8 @@
                     wg[j, r, hcol[0]] = a.astype(BF16)
 
             for k in range(1, nqy):
-                n = k - 1
                 src = wg.at[j, slot(pos_y(k), qx), hcol[0]]
-                batch.append(remote(src, r2a.at[i, k - 1], q2s.at[i, n], q2r.at[i, n], dev_y(k)))
+                remote(src, r2a.at[i, k - 1], q2s, q2r.at[i], dev_y(k))
         else:
             @pl.loop(0, nqx * rows // 16)
             def _(g):
@@ -327,18 +314,14 @@
                 wg[j, r, hcol[1]] = a.astype(BF16)
 
             for k in range(1, nqx):
-                n = nqy - 1 + k - 1
                 src = wg.at[j, slot(qy, pos_x(k)), hcol[1]]
-                batch.append(remote(src, r2b.at[i, k - 1], q2s.at[i, n], q2r.at[i, n], dev_x(k)))
-        q2_copies[i, h] = batch
-
-    z_copies = []
+                remote(src, r2b.at[i, k - 1], q2s, q2r.at[i], dev_x(k))
+
+    sent.append((zs, zsd))
 
     def final(i):
         j = dest(i)
-        for h in range(2):
-            for copy in q2_copies[i, h]:
-                copy.wait_recv()
+        arrived(chunks(na), q2r.at[i])
 
         @pl.loop(0, rows // 16)
         def _(g):
@@ -354,13 +337,13 @@
                     gsum[r, part] = a
 
         if i < nt - 1:
-            z_copies.append(remote(zs.at[i], rz.at[i], zsd.at[i], zr.at[i], (dp, j)))
+            remote(zs.at[i], rz.at[i], zsd, zr, (dp, j))
 
     uc = min(256, cols)
 
     def upstream(i):
         b = block(i)
-        third[i].wait_recv()
+        arrived(wf.at[b, pl.ds(mine, half)], a3r.at[i])
 
         @pl.loop(0, cols // uc)
         def _(h):
@@ -387,18 +370,17 @@
     early = min(4, len(units))
     for n, unit in enumerate(units):
         product(*unit)
-        if n == 1:
-            own.wait()
-            for copy in first:
-                copy.wait_recv()
-            pass_on(t, 0, 1)
-            pass_on(t, 1, 1)
         if n == len(units) - 1:
             relay(1, 1)
         if n > 0:
             pair_sum(*units[n - 1])
             if n <= early:
                 reduce_first(*units[n - 1])
+        if n == 2:
+            own.wait()
+            arrived(chunks(na), a1r)
+            pass_on(t, 0, 1)
+            pass_on(t, 1, 1)
         if n == early:
             relay(1, 0)
     pair_sum(*units[-1])
@@ -414,6 +396,8 @@
     both_middle(0)
     both_middle(1)
     final(0)
+    if nt > 3:
+        relay(2, 0)
     for i in range(2, nt):
         both_middle(i)
         if i == nt - 1:
@@ -421,12 +405,11 @@
             spread(1)
         final(i - 1)
         if i > 2:
-            relay(i - 1, 0)
+            relay(i - 1, 1)
             if i < nt - 1:
-                relay(i - 1, 1)
+                relay(i, 0)
     final(nt - 1)
-    for copy in z_copies:
-        copy.wait_recv()
+    arrived(rz, zr)
 
     nsend[0] = jnp.zeros((8, 128), F32)
 
@@ -453,13 +436,11 @@
     for step, devs in enumerate(groups):
         if step > 0:
             nsend[step] = v
-        batch = [
-            remote(nsend.at[step], nrecv.at[base + n], nss.at[base + n], nsr.at[base + n], dev)
-            for n, dev in enumerate(devs)
-        ]
+        for n, dev in enumerate(devs):
+            remote(nsend.at[step], nrecv.at[base + n], nss.at[step], nsr.at[step], dev)
+        batch = nrecv.at[pl.ds(base, len(devs))]
+        sent.append((batch, nss.at[step]))
         if step == 0:
-            if nt > 2:
-                relay(nt - 2, 1)
             for i in range(2, nt - 1):
                 spread(i)
             gather_third(0)
@@ -468,9 +449,9 @@
             gather_third(1)
             relay(nt - 1, 0)
             relay(nt - 1, 1)
-            spread(nt - 1)
-        for n, copy in enumerate(batch):
-            copy.wait_recv()
+            spread(nt - 1, (True,))
+        arrived(batch, nsr.at[step])
+        for n in range(len(devs)):
             v = v + nrecv[base + n]
         base += len(devs)
     total_square = jnp.sum(jnp.sum(v, axis=1, keepdims=True), axis=0, keepdims=True)
@@ -497,40 +478,34 @@
     def piece_of(yy, xx, part):
         return nwb.at[yy * nqx + xx, pl.ds(nat, rows), part]
 
-    w_first = []
     for k in range(1, nqx):
         part = piece_of(qy, qx, hcol[0])
-        w_first.append(remote(part, part, ws.at[k - 1], wr.at[k - 1], dev_x(k)))
+        remote(part, part, ws, wr, dev_x(k))
     for k in range(1, nqy):
-        n = nqx - 1 + k - 1
         part = piece_of(qy, qx, hcol[1])
-        w_first.append(remote(part, part, ws.at[n], wr.at[n], dev_y(k)))
-
+        remote(part, part, ws, wr, dev_y(k))
+    sent.append((chunks(na), ws))
+
+    spread(nt - 1, (False,))
     for i in range(1, nt - 1):
-        gather_third(i + 1)
+        if i < nt - 2:
+            gather_third(i + 1)
         upstream(i)
 
-    for copy in w_first:
-        copy.wait_recv()
-    w_second = []
-    for k in range(1, nqy):
-        for xx in range(nqx):
-            part = piece_of(qy, xx, hcol[0])
-            n = len(w_second)
-            w_second.append(remote(part, part, vs.at[n], vr.at[n], dev_y(k)))
-    for k in range(1, nqx):
-        for yy in range(nqy):
-            part = piece_of(yy, qx, hcol[1])
-            n = len(w_second)
-            w_second.append(remote(part, part, vs.at[n], vr.at[n], dev_x(k)))
-    nw1 = len(w_second)
-    lasts = [
-        remote(part, part, us.at[n], ur.at[n], (mate, t))
-        for n, part in enumerate(
-            [piece_of(qy, pos_x(m), hcol[0]) for m in range(nqx)]
-            + [piece_of(pos_y(m), qx, hcol[1]) for m in range(nqy)]
-        )
-    ]
+    arrived(chunks(na), wr)
+    for m in range(max(nqx, nqy)):
+        for k in range(1, nqy if m < nqx else 1):
+            part = piece_of(qy, pos_x(m), hcol[0])
+            remote(part, part, vs, vr, dev_y(k))
+        for k in range(1, nqx if m < nqy else 1):
+            part = piece_of(pos_y(m), qx, hcol[1])
+            remote(part, part, vs, vr, dev_x(k))
+    sent.append((chunks(nw2), vs))
+    gather_third(nt - 1)
+    early_parts = [(qy, pos_x(m), hcol[0]) for m in range(nqx)] + [(pos_y(m), qx, hcol[1]) for m in range(nqy)]
+    for place in early_parts:
+        part = piece_of(*place)
+        remote(part, part, us, ur, (mate, t))
     upstream(nt - 1)
 
     for k in range(ntile):
@@ -538,47 +513,50 @@
         down = ssq[lanes, :1] * (jnp.sum(cross[lanes, :], axis=1, keepdims=True) / width)
         cross[lanes, :] = jnp.broadcast_to(down, (tile, 128))
 
-    def finish(a, b):
-        @pl.loop(a // 16, b // 16)
+    arrived(chunks(nw2), vr)
+    late_parts = [(pos_y(k), pos_x(m), hcol[0]) for k in range(1, nqy) for m in range(nqx)]
+    late_parts += [(pos_y(m), pos_x(k), hcol[1]) for k in range(1, nqx) for m in range(nqy)]
+    for place in late_parts:
+        part = piece_of(*place)
+        remote(part, part, us, ur, (mate, t))
+    whole = nwb.at[:, pl.ds(nat, rows)]
+    sent.append((whole, us))
+    arrived(whole, ur)
+    for like, sem in sent:
+        left(like, sem)
+    for side, b, here in line_sent:
+        there = t + 1 < nt if side == 0 else t >= 1
+
+        @pl.when(jnp.logical_and(here, there))
+        def _(side=side, b=b):
+            left(chunks(2 + na), zfs.at[side, b])
+
+
+def write_out(grad, x, down, nwb, nf, ns, grad_out, nw_out, nf_out, ns_out, done, sem, gsem):
+    tokens, width = x.shape
+    tile = min(32, tokens)
+    small = [
+        pltpu.make_async_copy(src, dst, sem.at[n])
+        for n, (src, dst) in enumerate(((nwb, nw_out), (nf, nf_out), (ns, ns_out)))
+    ]
+    copies = list(small)
+    for k in range(tokens // tile):
+        if k == 1:
+            for copy in small:
+                copy.start()
+
+        @pl.loop(0, tile // 16)
         def _(g):
-            r = pl.ds(pl.multiple_of(g * 16, 16), 16)
-            down = cross[r, :]
+            r = pl.ds(pl.multiple_of(k * tile + g * 16, 16), 16)
+            factor = down[r, :]
             for n in range(width // 128):
                 col = slice(n * 128, (n + 1) * 128)
-                grad[r, col] = (grad[r, col].astype(F32) - down * x[r, col].astype(F32)).astype(BF16)
-
-    finish(0, tokens // 2)
-    for copy in w_second:
-        copy.wait_recv()
-    lasts += [
-        remote(part, part, vs.at[nw1 + n], vr.at[nw1 + n], (mate, t))
-        for n, part in enumerate(
-            [piece_of(pos_y(k), pos_x(m), hcol[0]) for k in range(1, nqy) for m in range(nqx)]
-            + [piece_of(pos_y(m), pos_x(k), hcol[1]) for k in range(1, nqx) for m in range(nqy)]
-        )
-    ]
-    finish(tokens // 2, tokens)
-    for copy in lasts:
-        copy.wait_recv()
-    for _, sent in sends:
-        sent.wait_send()
-    for side, b, here in line_sent:
-        there = t + 1 < nt if side == 0 else t >= 1
-
-        @pl.when(jnp.logical_and(here, there))
-        def _(side=side, b=b):
-            for p in range(2):
-                for copy in line_pieces(b, side, p, (dp, t)):
-                    copy.wait_send()
-
-
-def write_out(a, b, c, d, a_out, b_out, c_out, d_out, sem):
-    copies = [
-        pltpu.make_async_copy(src, dst, sem.at[n])
-        for n, (src, dst) in enumerate(((a, a_out), (b, b_out), (c, c_out), (d, d_out)))
-    ]
-    for copy in copies:
+                done[r, col] = (grad[r, col].astype(F32) - factor * x[r, col].astype(F32)).astype(BF16)
+
+        piece = pl.ds(k * tile, tile)
+        copy = pltpu.make_async_copy(done.at[piece], grad_out.at[piece], gsem.at[k])
         copy.start()
+        copies.append(copy)
     for copy in copies:
         copy.wait()
 
@@ -606,7 +584,6 @@
     nw2 = nx1 + (nqy - 1) * nqx
     nn = ndp - 1 + nt - 1
     scratch = [
-        pltpu.VMEM((tokens, width), BF16),
         pltpu.VMEM((tokens, features), BF16),
         pltpu.VMEM((ntile, tile), jnp.int32),
         pltpu.VMEM((width // 128, 128), BF16),
@@ -617,7 +594,6 @@
         pltpu.VMEM((tokens, features), BF16),
         pltpu.VMEM((features, tokens), BF16),
         pltpu.VMEM((features, tokens), BF16),
-        pltpu.VMEM((tokens, 128), F32),
         pltpu.VMEM((tokens, 128), F32),
         pltpu.VMEM((nt, features, cols), BF16),
         pltpu.VMEM((nt, features, cols), BF16),
@@ -632,32 +608,34 @@
         pltpu.VMEM((2, 8, 128), F32),
         pltpu.VMEM((nn, 8, 128), F32),
         dma((7,)), dma((ntile,)),
-        dma((na,)), dma((na,)),
-        dma((2, nt, 1 + na)), dma((nt, 1 + na)),
-        dma((nt, nw2)), dma((nt, nw2)),
-        dma((nt,)), dma((nt,)),
-        dma((2 * nt,)), dma((2 * nt,)),
-        dma((nt, nx1 + nqy - 1)), dma((nt, nx1 + nqy - 1)),
-        dma((nt, na)), dma((nt, na)),
-        dma((nt - 1,)), dma((nt - 1,)),
-        dma((nn,)), dma((nn,)),
-        dma((na,)), dma((na,)),
-        dma((2 * nw2,)), dma((2 * nw2,)),
-        dma((nqx + nqy,)), dma((nqx + nqy,)),
+        dma, dma,
+        dma((2, nt)), dma((nt, 2)),
+        dma, dma((nt,)),
+        dma, dma((nt,)),
+        dma, dma((2 * nt,)),
+        dma, dma((nt, 2)),
+        dma, dma((nt,)),
+        dma, dma,
+        dma((2,)), dma((2,)),
+        dma, dma,
+        dma, dma,
+        dma, dma,
     ]
     results = pl.pallas_call(
         functools.partial(kernel, ndp, nt, nqx),
         out_shape=(
             pltpu.VMEM((tokens, width), BF16),
+            pltpu.VMEM((tokens, width), BF16),
+            pltpu.VMEM((tokens, 128), F32),
             pltpu.VMEM((nq, 2 * rows, cols), BF16),
             pltpu.VMEM((rows, cols), F32),
             pltpu.VMEM((rows, cols), F32),
         ),
         in_specs=[any_spec] * 8,
-        out_specs=(vmem, vmem, vmem, vmem),
+        out_specs=(vmem,) * 6,
         scratch_shapes=scratch,
         compiler_params=pltpu.CompilerParams(
-            collective_id=0, has_side_effects=True, vmem_limit_bytes=48 * 2**20
+            collective_id=0, has_side_effects=True, vmem_limit_bytes=42 * 2**20
         ),
     )(
         norm_input, key_grad, positions.reshape(ntile, tile), norm_gain.reshape(width // 128, 128),
@@ -666,11 +644,11 @@
     results = [pltpu.with_memory_space_constraint(r, pltpu.VMEM) for r in results]
     input_grad, new_weight, new_first, new_second = pl.pallas_call(
         write_out,
-        out_shape=[jax.ShapeDtypeStruct(r.shape, r.dtype) for r in results],
-        in_specs=[vmem] * 4,
+        out_shape=[jax.ShapeDtypeStruct(results[n].shape, results[n].dtype) for n in (0, 3, 4, 5)],
+        in_specs=[vmem] * 6,
         out_specs=[any_spec] * 4,
-        scratch_shapes=[dma((4,))],
-        compiler_params=pltpu.CompilerParams(vmem_limit_bytes=2**20),
+        scratch_shapes=[pltpu.VMEM((tokens, width), BF16), dma((3,)), dma((tokens // min(32, tokens),))],
+        compiler_params=pltpu.CompilerParams(vmem_limit_bytes=10 * 2**20),
     )(*results)
     return (input_grad, new_weight.reshape(features, cols), new_first, new_second)
 

time: 88.5 us -> 83.6 us (0.945)
  Pallas kernels: 87.7 us -> 82.8 us
    pallas_call x1, Pallas kernels: 83.4 us -> 78.3 us  [body(): pl.pallas_call(functools.partial(kernel, ndp, nt, nqx), out_shape=(pltpu....]
where the time goes in v4:
time: 83.6 us; the launch traced here: 83.5 us
  Pallas kernels  82.8 us (99%)
    pallas_call x1, Pallas kernels, body(): pl.pallas_call(functools.partial(kernel, ndp, nt, nqx), out_shape=(pltpu....  78.3 us
    pallas_call x1, Pallas kernels, body(): pl.pallas_call(write_out, out_shape=[jax.ShapeDtypeStruct(results[n].shap...  4.48 us

profile of v4, /device:TPU:0, one launch (start us, length us, event | category | flops | bytes accessed | tf_op | source)
XLA Modules:
  0.0 83.5 jit_solution(13941003208120152801)
XLA Ops:
  0.6 78.3 %shard_map.111 = (bf16[512,8192]{1,0:T(8,128)(2,1)S(1)}, bf16[512,8192]{1,0:T(8,128)(2,1)S(1)}, f32[512,128]{1,0:T(8,128)S(1)}, bf16[4,128,2048]{2,1,0:T(8,128)(...) custom-call(bf16[512,8192]{1,0:T(8,128)(2,1)} %x_hbm.1, bf16[512,512]{1,0:T(8,128)(2,1)} %kg_hbm.1, ...), custom_call_target="tpu_custom_call" | custom-call | tf_op jit(solution)/shard_map/pallas_call | solution.py:624
  79.0 4.5 %shard_map.112 = (bf16[512,8192]{1,0:T(8,128)(2,1)}, bf16[4,128,2048]{2,1,0:T(8,128)(2,1)}, f32[64,2048]{1,0:T(8,128)}, f32[64,2048]{1,0:T(8,128)}) custom-call(bf16[512,8192]{1,0:T(8,128)(2,1)S(1)} %get-tuple-element.14.grad, bf16[512,8192]{1,0:T(8,128)(2,1)S(1)} %get-tuple-element.15.x, f32[512,128]{1,0:T(8,128)S(1)} %get-tuple-element.16.down, ...), custom_call_target="tpu_custom_call" | custom-call | tf_op jit(solution)/shard_map/pallas_call | solution.py:645

commit v5 on v4

--- a/solution.py
+++ b/solution.py
@@ -30,7 +30,7 @@
     grad, x, cross, nwb, nf, ns,
     kg, pos, gain_in, freq, m1, m2, gain, kb, kbt, sks, ssq,
     wf, wg, rcore, r1a, r1b, r2a, r2b, zs, rz, gsum, nsend, nrecv,
-    isem, xsem, a1s, a1r, zfs, zfr, b3s, b3r, a3s, a3r, cs, cr, qs, qr, q2s, q2r,
+    isem, xsem, a1s, a1r, zfs, zfr, b3s, b3r, b4s, p2s, p2r, a3s, a3r, cs, cr, qs, qr, q2s, q2r,
     zsd, zr, nss, nsr, ws, wr, vs, vr, us, ur,
 ):
     nq = ndp // 2
@@ -105,7 +105,7 @@
         if i == 0:
             return t
         d = (i + 1) // 2
-        both = t - d if i % 2 else t + d
+        both = t + (d if i % 2 else -d) * jnp.where(low, -1, 1)
         return jnp.where(i <= 2 * near, both, jnp.where(low, i, nt - 1 - i))
 
     def local(src, dst, sem):
@@ -174,9 +174,10 @@
                     if (m == 0) in near:
                         part = wf.at[b, place, hcol[h]]
                         src = w_hbm.at[:, hcol[h]] if i == 0 and m == 0 else part
-                        remote(src, part, b3s, b3r.at[i], dev(k))
-
-    sent.append((layers(nw2), b3s))
+                        remote(src, part, b4s if i == nt - 1 else b3s, b3r.at[i], dev(k))
+
+    sent.append((wg.at[pl.ds(0, nt - 1), pl.ds(0, nw2 * rows), hcol[0]], b3s))
+    sent.append((chunks(nw2 - na), b4s))
     spread(0, (True,))
 
     def line_pieces(b, side, p, dev):
@@ -212,8 +213,39 @@
         def _(side=side, to=to):
             describe(w_hbm, wf.at[t, my_rows], zfs.at[side, t], zfr.at[t, 0], (dp, to)).start()
 
+    def other_parts(b):
+        parts = [wf.at[b, slot(pos_y(k), qx), hcol[0]] for k in range(1, nqy)]
+        return parts + [wf.at[b, slot(qy, pos_x(k)), hcol[1]] for k in range(1, nqx)]
+
+    half_line = nt // 2
+    middle_low = t == half_line - 1
+    middle_high = t == half_line
+
+    def cross_over():
+        for here, b, far in (
+            (middle_low, 0, [half_line + n for n in range(half_line)]),
+            (middle_high, nt - 1, [half_line - 1 - n for n in range(half_line)]),
+        ):
+            @pl.when(here)
+            def _(b=b, far=far):
+                for n, to in enumerate(far):
+                    for part in other_parts(b):
+                        remote(part, part, p2s.at[n], p2r, (dp, to))
+
+    def crossed_over():
+        @pl.when(jnp.logical_or(middle_low, middle_high))
+        def _():
+            for n in range(half_line):
+                left(chunks(na), p2s.at[n])
+
     def gather_third(i):
-        arrived(chunks(nw2), b3r.at[i])
+        if i == nt - 1:
+            arrived(chunks(na), p2r)
+            arrived(chunks(nw2 - na), b3r.at[i])
+        else:
+            arrived(chunks(nw2), b3r.at[i])
+        if i == nt - 3 and i > 1:
+            cross_over()
         part = wf.at[block(i), pl.ds(mine, half)]
         remote(part, part, a3s, a3r.at[i], (mate, t))
 
@@ -401,17 +433,16 @@
     for i in range(2, nt):
         both_middle(i)
         if i == nt - 1:
+            spread(1)
             spread(0, (False,))
-            spread(1)
         final(i - 1)
-        if i > 2:
+        if 2 < i < nt - 1:
             relay(i - 1, 1)
-            if i < nt - 1:
-                relay(i, 0)
+            relay(i, 0)
     final(nt - 1)
     arrived(rz, zr)
 
-    nsend[0] = jnp.zeros((8, 128), F32)
+    nsend[...] = jnp.zeros_like(nsend)
 
     @pl.loop(0, rows // 16)
     def _(g):
@@ -421,40 +452,30 @@
             a = a + rz[i, r, :].astype(F32)
         gsum[r, :] = a
         a = a * a
-        a = a[:8] + a[8:]
         total = a[:, :128]
         for k in range(1, cols // 128):
             total = total + a[:, k * 128 : (k + 1) * 128]
-        nsend[0] += total
-
-    v = nsend[0]
-    base = 0
-    groups = (
-        [((dp + k) % ndp, t) for k in range(1, ndp)],
-        [(dp, (t + k) % nt) for k in range(1, nt)],
-    )
-    for step, devs in enumerate(groups):
-        if step > 0:
-            nsend[step] = v
-        for n, dev in enumerate(devs):
-            remote(nsend.at[step], nrecv.at[base + n], nss.at[step], nsr.at[step], dev)
-        batch = nrecv.at[pl.ds(base, len(devs))]
-        sent.append((batch, nss.at[step]))
-        if step == 0:
-            for i in range(2, nt - 1):
-                spread(i)
-            gather_third(0)
-        else:
-            upstream(0)
-            gather_third(1)
-            relay(nt - 1, 0)
-            relay(nt - 1, 1)
-            spread(nt - 1, (True,))
-        arrived(batch, nsr.at[step])
-        for n in range(len(devs)):
-            v = v + nrecv[base + n]
-        base += len(devs)
-    total_square = jnp.sum(jnp.sum(v, axis=1, keepdims=True), axis=0, keepdims=True)
+        nsend[...] += jnp.sum(total, axis=0, keepdims=True)
+
+    n = 0
+    for b in reversed(range(nt)):
+        for a in range(ndp):
+            if a or b:
+                remote(nsend, nrecv.at[n], nss, nsr, ((dp + a) % ndp, (t + b) % nt))
+                n += 1
+    sent.append((nrecv, nss))
+    if nt > 3:
+        relay(nt - 2, 1)
+    gather_third(1)
+    if nt - 3 == 1:
+        cross_over()
+    for i in range(2, nt - 1):
+        spread(i)
+    gather_third(0)
+    upstream(1)
+    arrived(nrecv, nsr)
+    v = nsend[...] + jnp.sum(nrecv[...], axis=0)
+    total_square = jnp.sum(v, axis=1, keepdims=True)
     limit = math.sqrt(kbt.shape[0] * width)
     clip = jnp.minimum(1.0, limit / (jnp.sqrt(total_square) + 1e-06))
     nat = pl.multiple_of(c * rows, rows)
@@ -486,26 +507,30 @@
         remote(part, part, ws, wr, dev_y(k))
     sent.append((chunks(na), ws))
 
+    upstream(0)
+    relay(nt - 1, 0)
+    relay(nt - 1, 1)
     spread(nt - 1, (False,))
-    for i in range(1, nt - 1):
+    for i in range(2, nt - 1):
+        gather_third(i)
         if i < nt - 2:
-            gather_third(i + 1)
-        upstream(i)
+            upstream(i)
 
     arrived(chunks(na), wr)
     for m in range(max(nqx, nqy)):
         for k in range(1, nqy if m < nqx else 1):
             part = piece_of(qy, pos_x(m), hcol[0])
-            remote(part, part, vs, vr, dev_y(k))
+            remote(part, part, vs, vr.at[min(m, 1)], dev_y(k))
         for k in range(1, nqx if m < nqy else 1):
             part = piece_of(pos_y(m), qx, hcol[1])
-            remote(part, part, vs, vr, dev_x(k))
+            remote(part, part, vs, vr.at[min(m, 1)], dev_x(k))
     sent.append((chunks(nw2), vs))
-    gather_third(nt - 1)
     early_parts = [(qy, pos_x(m), hcol[0]) for m in range(nqx)] + [(pos_y(m), qx, hcol[1]) for m in range(nqy)]
     for place in early_parts:
         part = piece_of(*place)
         remote(part, part, us, ur, (mate, t))
+    upstream(nt - 2)
+    gather_third(nt - 1)
     upstream(nt - 1)
 
     for k in range(ntile):
@@ -513,17 +538,23 @@
         down = ssq[lanes, :1] * (jnp.sum(cross[lanes, :], axis=1, keepdims=True) / width)
         cross[lanes, :] = jnp.broadcast_to(down, (tile, 128))
 
-    arrived(chunks(nw2), vr)
-    late_parts = [(pos_y(k), pos_x(m), hcol[0]) for k in range(1, nqy) for m in range(nqx)]
-    late_parts += [(pos_y(m), pos_x(k), hcol[1]) for k in range(1, nqx) for m in range(nqy)]
-    for place in late_parts:
-        part = piece_of(*place)
-        remote(part, part, us, ur, (mate, t))
+    for late, count in ((0, na), (1, nw2 - na)):
+        arrived(chunks(count), vr.at[late])
+        late_parts = [
+            (pos_y(k), pos_x(m), hcol[0]) for k in range(1, nqy) for m in range(nqx) if min(m, 1) == late
+        ]
+        late_parts += [
+            (pos_y(m), pos_x(k), hcol[1]) for k in range(1, nqx) for m in range(nqy) if min(m, 1) == late
+        ]
+        for place in late_parts:
+            part = piece_of(*place)
+            remote(part, part, us, ur, (mate, t))
     whole = nwb.at[:, pl.ds(nat, rows)]
     sent.append((whole, us))
     arrived(whole, ur)
     for like, sem in sent:
         left(like, sem)
+    crossed_over()
     for side, b, here in line_sent:
         there = t + 1 < nt if side == 0 else t >= 1
 
@@ -582,7 +613,7 @@
     na = nqx + nqy - 2
     nx1 = (nqx - 1) * nqy
     nw2 = nx1 + (nqy - 1) * nqx
-    nn = ndp - 1 + nt - 1
+    nn = ndp * nt - 1
     scratch = [
         pltpu.VMEM((tokens, features), BF16),
         pltpu.VMEM((ntile, tile), jnp.int32),
@@ -605,20 +636,21 @@
         pltpu.VMEM((nt - 1, rows, cols), BF16),
         pltpu.VMEM((nt - 1, rows, cols), BF16),
         pltpu.VMEM((rows, cols), F32),
-        pltpu.VMEM((2, 8, 128), F32),
-        pltpu.VMEM((nn, 8, 128), F32),
+        pltpu.VMEM((1, 128), F32),
+        pltpu.VMEM((nn, 1, 128), F32),
         dma((7,)), dma((ntile,)),
         dma, dma,
         dma((2, nt)), dma((nt, 2)),
-        dma, dma((nt,)),
+        dma, dma((nt,)), dma,
+        dma((nt // 2,)), dma,
         dma, dma((nt,)),
         dma, dma((2 * nt,)),
         dma, dma((nt, 2)),
         dma, dma((nt,)),
         dma, dma,
-        dma((2,)), dma((2,)),
         dma, dma,
         dma, dma,
+        dma, dma((2,)),
         dma, dma,
     ]
     results = pl.pallas_call(

time: 83.6 us -> 80.6 us (0.964)
  Pallas kernels: 82.8 us -> 79.8 us
    pallas_call x1, Pallas kernels: 78.3 us -> 75.4 us  [body(): pl.pallas_call(functools.partial(kernel, ndp, nt, nqx), out_shape=(pltpu....]
where the time goes in v5:
time: 80.6 us; the launch traced here: 80.5 us
  Pallas kernels  79.8 us (99%)
    pallas_call x1, Pallas kernels, body(): pl.pallas_call(functools.partial(kernel, ndp, nt, nqx), out_shape=(pltpu....  75.4 us
    pallas_call x1, Pallas kernels, body(): pl.pallas_call(write_out, out_shape=[jax.ShapeDtypeStruct(results[n].shap...  4.48 us

profile of v5, /device:TPU:0, one launch (start us, length us, event | category | flops | bytes accessed | tf_op | source)
XLA Modules:
  0.0 80.5 jit_solution(11443820544913673789)
XLA Ops:
  0.6 75.4 %shard_map.111 = (bf16[512,8192]{1,0:T(8,128)(2,1)S(1)}, bf16[512,8192]{1,0:T(8,128)(2,1)S(1)}, f32[512,128]{1,0:T(8,128)S(1)}, bf16[4,128,2048]{2,1,0:T(8,128)(...) custom-call(bf16[512,8192]{1,0:T(8,128)(2,1)} %x_hbm.1, bf16[512,512]{1,0:T(8,128)(2,1)} %kg_hbm.1, ...), custom_call_target="tpu_custom_call" | custom-call | tf_op jit(solution)/shard_map/pallas_call | solution.py:656
  76.0 4.5 %shard_map.112 = (bf16[512,8192]{1,0:T(8,128)(2,1)}, bf16[4,128,2048]{2,1,0:T(8,128)(2,1)}, f32[64,2048]{1,0:T(8,128)}, f32[64,2048]{1,0:T(8,128)}) custom-call(bf16[512,8192]{1,0:T(8,128)(2,1)S(1)} %get-tuple-element.14.grad, bf16[512,8192]{1,0:T(8,128)(2,1)S(1)} %get-tuple-element.15.x, f32[512,128]{1,0:T(8,128)S(1)} %get-tuple-element.16.down, ...), custom_call_target="tpu_custom_call" | custom-call | tf_op jit(solution)/shard_map/pallas_call | solution.py:677

commit v6 on v5

--- a/solution.py
+++ b/solution.py
@@ -126,10 +126,122 @@
     m2_in = local(m2_hbm, m2, isem.at[6])
 
     barrier = pltpu.get_barrier_semaphore()
-    for k in range(1, ndp):
-        pl.semaphore_signal(barrier, inc=1, device_id=((dp + k) % ndp, t), device_id_type=MESH)
-    for k in range(1, nt):
-        pl.semaphore_signal(barrier, inc=1, device_id=(dp, (t + k) % nt), device_id_type=MESH)
+
+    def greet(dev):
+        pl.semaphore_signal(barrier, inc=1, device_id=dev, device_id_type=MESH)
+
+    greet((mate, t))
+    for k in range(1, nqx):
+        greet(dev_x(k))
+    for k in range(1, nqy):
+        greet(dev_y(k))
+    met = 1 + (nqx - 1) + (nqy - 1)
+    if nt > 4:
+        for k in range(1, nt):
+            greet((dp, (t + k) % nt))
+        pl.semaphore_wait(barrier, met + nt - 1)
+    else:
+        pl.when(t >= 1)(lambda: greet((dp, t - 1)))
+        pl.when(t + 1 < nt)(lambda: greet((dp, t + 1)))
+        pl.semaphore_wait(barrier, met + jnp.where(t >= 1, 1, 0) + jnp.where(t + 1 < nt, 1, 0))
+
+
+    na = nqx + nqy - 2
+    nx1 = (nqx - 1) * nqy
+    ny1 = (nqy - 1) * nqx
+    nw2 = nx1 + ny1
+    own.wait()
+    for k in range(1, nqx):
+        remote(wf.at[t, my_rows, hcol[0]], wf.at[t, my_rows, hcol[0]], a1s, a1r, dev_x(k))
+    for k in range(1, nqy):
+        remote(wf.at[t, my_rows, hcol[1]], wf.at[t, my_rows, hcol[1]], a1s, a1r, dev_y(k))
+    sent.append((chunks(na), a1s))
+
+    def spread(i, near=(False, True)):
+        b = block(i)
+        for h, count, other, dev in ((0, nqx, nqy, dev_y), (1, nqy, nqx, dev_x)):
+            for k in range(1, other):
+                for m in range(count):
+                    place = slot(qy, pos_x(m)) if h == 0 else slot(pos_y(m), qx)
+                    if (m == 0) in near:
+                        part = wf.at[b, place, hcol[h]]
+                        remote(part, part, b4s if i == nt - 1 else b3s, b3r.at[i], dev(k))
+
+    sent.append((wg.at[pl.ds(0, nt - 1), pl.ds(0, nw2 * rows), hcol[0]], b3s))
+    sent.append((chunks(nw2 - na), b4s))
+    spread(0, (True,))
+
+    def line_pieces(b, side, p, dev):
+        if p == 0:
+            parts = [wf.at[b, my_rows]]
+        else:
+            parts = [wf.at[b, slot(qy, pos_x(k)), hcol[0]] for k in range(1, nqx)]
+            parts += [wf.at[b, slot(pos_y(k), qx), hcol[1]] for k in range(1, nqy)]
+        return [describe(part, part, zfs.at[side, b], zfr.at[b, p], dev) for part in parts]
+
+    def pass_on(b, side, p):
+        to, there = (t + 1, t + 1 < nt) if side == 0 else (t - 1, t >= 1)
+
+        @pl.when(there)
+        def _():
+            for copy in line_pieces(b, side, p, (dp, to)):
+                copy.start()
+
+    line_sent = [(0, t, t >= 0), (1, t, t >= 0)]
+
+    def relay(d, p):
+        for side, b, here in ((0, t - d, t - d >= 0), (1, t + d, t + d < nt)):
+            @pl.when(here)
+            def _(side=side, b=b):
+                arrived(chunks(2 if p == 0 else na), zfr.at[b, p])
+                pass_on(b, side, p)
+
+            if p == 0:
+                line_sent.append((side, b, here))
+
+    for side, to, there in ((0, t + 1, t + 1 < nt), (1, t - 1, t >= 1)):
+        @pl.when(there)
+        def _(side=side, to=to):
+            describe(wf.at[t, my_rows], wf.at[t, my_rows], zfs.at[side, t], zfr.at[t, 0], (dp, to)).start()
+
+    def other_parts(b):
+        parts = [wf.at[b, slot(pos_y(k), qx), hcol[0]] for k in range(1, nqy)]
+        return parts + [wf.at[b, slot(qy, pos_x(k)), hcol[1]] for k in range(1, nqx)]
+
+    half_line = nt // 2
+    middle_low = t == half_line - 1
+    middle_high = t == half_line
+
+    def cross_over():
+        for here, b, far in (
+            (middle_low, 0, [half_line + n for n in range(half_line)]),
+            (middle_high, nt - 1, [half_line - 1 - n for n in range(half_line)]),
+        ):
+            @pl.when(here)
+            def _(b=b, far=far):
+                for n, to in enumerate(far):
+                    for part in other_parts(b):
+                        remote(part, part, p2s.at[n], p2r, (dp, to))
+
+    def crossed_over():
+        @pl.when(jnp.logical_or(middle_low, middle_high))
+        def _():
+            for n in range(half_line):
+                left(chunks(na), p2s.at[n])
+
+    def gather_third(i):
+        if i == nt - 1:
+            arrived(chunks(na), p2r)
+            arrived(chunks(nw2 - na), b3r.at[i])
+        else:
+            arrived(chunks(nw2), b3r.at[i])
+        if i == nt - 3 and i > 1:
+            cross_over()
+        part = wf.at[block(i), pl.ds(mine, half)]
+        remote(part, part, a3s, a3r.at[i], (mate, t))
+
+    sent.append((wg.at[:, pl.ds(0, half)], a3s))
+
     cross[...] = jnp.zeros_like(cross)
     kg_in.wait()
     pos_in.wait()
@@ -153,104 +265,6 @@
                         m * rows : (m + 1) * rows
                     ]
 
-    pl.semaphore_wait(barrier, ndp - 1 + nt - 1)
-
-    na = nqx + nqy - 2
-    nx1 = (nqx - 1) * nqy
-    ny1 = (nqy - 1) * nqx
-    nw2 = nx1 + ny1
-    for k in range(1, nqx):
-        remote(w_hbm.at[:, hcol[0]], wf.at[t, my_rows, hcol[0]], a1s, a1r, dev_x(k))
-    for k in range(1, nqy):
-        remote(w_hbm.at[:, hcol[1]], wf.at[t, my_rows, hcol[1]], a1s, a1r, dev_y(k))
-    sent.append((chunks(na), a1s))
-
-    def spread(i, near=(False, True)):
-        b = block(i)
-        for h, count, other, dev in ((0, nqx, nqy, dev_y), (1, nqy, nqx, dev_x)):
-            for k in range(1, other):
-                for m in range(count):
-                    place = slot(qy, pos_x(m)) if h == 0 else slot(pos_y(m), qx)
-                    if (m == 0) in near:
-                        part = wf.at[b, place, hcol[h]]
-                        src = w_hbm.at[:, hcol[h]] if i == 0 and m == 0 else part
-                        remote(src, part, b4s if i == nt - 1 else b3s, b3r.at[i], dev(k))
-
-    sent.append((wg.at[pl.ds(0, nt - 1), pl.ds(0, nw2 * rows), hcol[0]], b3s))
-    sent.append((chunks(nw2 - na), b4s))
-    spread(0, (True,))
-
-    def line_pieces(b, side, p, dev):
-        if p == 0:
-            parts = [wf.at[b, my_rows]]
-        else:
-            parts = [wf.at[b, slot(qy, pos_x(k)), hcol[0]] for k in range(1, nqx)]
-            parts += [wf.at[b, slot(pos_y(k), qx), hcol[1]] for k in range(1, nqy)]
-        return [describe(part, part, zfs.at[side, b], zfr.at[b, p], dev) for part in parts]
-
-    def pass_on(b, side, p):
-        to, there = (t + 1, t + 1 < nt) if side == 0 else (t - 1, t >= 1)
-
-        @pl.when(there)
-        def _():
-            for copy in line_pieces(b, side, p, (dp, to)):
-                copy.start()
-
-    line_sent = [(0, t, t >= 0), (1, t, t >= 0)]
-
-    def relay(d, p):
-        for side, b, here in ((0, t - d, t - d >= 0), (1, t + d, t + d < nt)):
-            @pl.when(here)
-            def _(side=side, b=b):
-                arrived(chunks(2 if p == 0 else na), zfr.at[b, p])
-                pass_on(b, side, p)
-
-            if p == 0:
-                line_sent.append((side, b, here))
-
-    for side, to, there in ((0, t + 1, t + 1 < nt), (1, t - 1, t >= 1)):
-        @pl.when(there)
-        def _(side=side, to=to):
-            describe(w_hbm, wf.at[t, my_rows], zfs.at[side, t], zfr.at[t, 0], (dp, to)).start()
-
-    def other_parts(b):
-        parts = [wf.at[b, slot(pos_y(k), qx), hcol[0]] for k in range(1, nqy)]
-        return parts + [wf.at[b, slot(qy, pos_x(k)), hcol[1]] for k in range(1, nqx)]
-
-    half_line = nt // 2
-    middle_low = t == half_line - 1
-    middle_high = t == half_line
-
-    def cross_over():
-        for here, b, far in (
-            (middle_low, 0, [half_line + n for n in range(half_line)]),
-            (middle_high, nt - 1, [half_line - 1 - n for n in range(half_line)]),
-        ):
-            @pl.when(here)
-            def _(b=b, far=far):
-                for n, to in enumerate(far):
-                    for part in other_parts(b):
-                        remote(part, part, p2s.at[n], p2r, (dp, to))
-
-    def crossed_over():
-        @pl.when(jnp.logical_or(middle_low, middle_high))
-        def _():
-            for n in range(half_line):
-                left(chunks(na), p2s.at[n])
-
-    def gather_third(i):
-        if i == nt - 1:
-            arrived(chunks(na), p2r)
-            arrived(chunks(nw2 - na), b3r.at[i])
-        else:
-            arrived(chunks(nw2), b3r.at[i])
-        if i == nt - 3 and i > 1:
-            cross_over()
-        part = wf.at[block(i), pl.ds(mine, half)]
-        remote(part, part, a3s, a3r.at[i], (mate, t))
-
-    sent.append((wg.at[:, pl.ds(0, half)], a3s))
-
     def sum_squares(k):
         x_in[k].wait()
 
@@ -404,12 +418,11 @@
         product(*unit)
         if n == len(units) - 1:
             relay(1, 1)
-        if n > 0:
-            pair_sum(*units[n - 1])
-            if n <= early:
-                reduce_first(*units[n - 1])
-        if n == 2:
-            own.wait()
+        for m in {1: (0, 1), 0: (), 2: ()}.get(n, (n - 1,)):
+            pair_sum(*units[m])
+            if m < early:
+                reduce_first(*units[m])
+        if n == 1:
             arrived(chunks(na), a1r)
             pass_on(t, 0, 1)
             pass_on(t, 1, 1)
@@ -570,12 +583,10 @@
         pltpu.make_async_copy(src, dst, sem.at[n])
         for n, (src, dst) in enumerate(((nwb, nw_out), (nf, nf_out), (ns, ns_out)))
     ]
+    for copy in small:
+        copy.start()
     copies = list(small)
     for k in range(tokens // tile):
-        if k == 1:
-            for copy in small:
-                copy.start()
-
         @pl.loop(0, tile // 16)
         def _(g):
             r = pl.ds(pl.multiple_of(k * tile + g * 16, 16), 16)

time: 80.6 us -> 80.3 us (level)
  no operation moved by 1% of the time
where the time goes in v6:
time: 80.3 us; the launch traced here: 80.2 us
  Pallas kernels  79.5 us (99%)
    pallas_call x1, Pallas kernels, body(): pl.pallas_call(functools.partial(kernel, ndp, nt, nqx), out_shape=(pltpu....  75.1 us
    pallas_call x1, Pallas kernels, body(): pl.pallas_call(write_out, out_shape=[jax.ShapeDtypeStruct(results[n].shap...  4.39 us

profile of v6, /device:TPU:0, one launch (start us, length us, event | category | flops | bytes accessed | tf_op | source)
XLA Modules:
  0.0 80.2 jit_solution(8975387874314540975)
XLA Ops:
  0.6 75.1 %shard_map.111 = (bf16[512,8192]{1,0:T(8,128)(2,1)S(1)}, bf16[512,8192]{1,0:T(8,128)(2,1)S(1)}, f32[512,128]{1,0:T(8,128)S(1)}, bf16[4,128,2048]{2,1,0:T(8,128)(...) custom-call(bf16[512,8192]{1,0:T(8,128)(2,1)} %x_hbm.1, bf16[512,512]{1,0:T(8,128)(2,1)} %kg_hbm.1, ...), custom_call_target="tpu_custom_call" | custom-call | tf_op jit(solution)/shard_map/pallas_call | solution.py:667
  75.8 4.4 %shard_map.112 = (bf16[512,8192]{1,0:T(8,128)(2,1)}, bf16[4,128,2048]{2,1,0:T(8,128)(2,1)}, f32[64,2048]{1,0:T(8,128)}, f32[64,2048]{1,0:T(8,128)}) custom-call(bf16[512,8192]{1,0:T(8,128)(2,1)S(1)} %get-tuple-element.14.grad, bf16[512,8192]{1,0:T(8,128)(2,1)S(1)} %get-tuple-element.15.x, f32[512,128]{1,0:T(8,128)S(1)} %get-tuple-element.16.down, ...), custom_call_target="tpu_custom_call" | custom-call | tf_op jit(solution)/shard_map/pallas_call | solution.py:688

commit v7 on v6

--- a/solution.py
+++ b/solution.py
@@ -292,42 +292,44 @@
 
     sent.append((wg.at[:, pl.ds(0, half)], cs))
 
-    def product(i, h):
+    def product(i, h, n, first=0, size=hc):
         j = dest(i)
-
-        @pl.loop(0, hc // cc)
-        def _(n):
-            off = pl.ds(pl.multiple_of(h * hc + n * cc, cc), cc)
-            col = pl.ds(pl.multiple_of(j * cols + h * hc + n * cc, cc), cc)
+        step = min(cc, size)
+
+        @pl.loop(0, size // step)
+        def _(m):
+            off = pl.ds(pl.multiple_of(h * hc + first + m * step, step), step)
+            col = pl.ds(pl.multiple_of(j * cols + h * hc + first + m * step, step), step)
             total = jnp.dot(sks[...], x[:, col], preferred_element_type=F32)
             wg[j, :, off] = (total * gain[:, col]).astype(BF16)
 
-        n = i * 2 + h
-        remote(wg.at[j, pl.ds(theirs, half), hcol[h]], rcore.at[j, :, hcol[h]], cs, cr.at[n], (mate, t))
-
-    def pair_sum(i, h):
+        part = pl.ds(h * hc + first, size)
+        remote(wg.at[j, pl.ds(theirs, half), part], rcore.at[j, :, part], cs, cr.at[n], (mate, t))
+
+    def pair_sum(i, h, n, first=0, size=hc):
         j = dest(i)
-        arrived(rcore.at[j, :, hcol[h]], cr.at[i * 2 + h])
+        part = pl.ds(h * hc + first, size)
+        arrived(rcore.at[j, :, part], cr.at[n])
 
         @pl.loop(0, half // 16)
         def _(g):
             r = pl.ds(pl.multiple_of(mine + g * 16, 16), 16)
             l = pl.ds(pl.multiple_of(g * 16, 16), 16)
-            a = wg[j, r, hcol[h]].astype(F32) + rcore[j, l, hcol[h]].astype(F32)
-            wg[j, r, hcol[h]] = a.astype(BF16)
-
-    def reduce_first(i, h):
+            a = wg[j, r, part].astype(F32) + rcore[j, l, part].astype(F32)
+            wg[j, r, part] = a.astype(BF16)
+
+    def reduce_first(i, h, first=0, size=hc):
         j = dest(i)
         if h == 0:
             for k in range(1, nqx):
                 for yy in range(nqy):
                     n = (k - 1) * nqy + yy
-                    src = wg.at[j, slot(yy, pos_x(k)), hcol[0]]
-                    remote(src, r1a.at[i, n], qs, qr.at[i, 0], dev_x(k))
+                    src = wg.at[j, slot(yy, pos_x(k)), pl.ds(first, size)]
+                    remote(src, r1a.at[i, n, :, pl.ds(first, size)], qs, qr.at[i, 0], dev_x(k))
         else:
             for k in range(1, nqy):
-                src = wg.at[j, band(pos_y(k)), hcol[1]]
-                remote(src, r1b.at[i, k - 1], qs, qr.at[i, 1], dev_y(k))
+                src = wg.at[j, band(pos_y(k)), pl.ds(hc + first, size)]
+                remote(src, r1b.at[i, k - 1, :, pl.ds(first, size)], qs, qr.at[i, 1], dev_y(k))
 
     sent.append((layers(nw2), qs))
     sent.append((layers(na), q2s))
@@ -412,17 +414,19 @@
             mean = jnp.sum(ssq[lanes, :], axis=1, keepdims=True) / width
             ssq[lanes, :] = jnp.broadcast_to(lax.rsqrt(mean + eps_norm), (tile, 128))
 
-    units = [(i, h) for i in range(nt) for h in range(2)]
-    early = min(4, len(units))
+    hq = hc // 2
+    units = [(0, 0, 0, 0, hq), (0, 1, 1, 0, hq), (0, 0, 2 * nt, hq, hq), (0, 1, 2 * nt + 1, hq, hq)]
+    units += [(i, h, i * 2 + h) for i in range(1, nt) for h in range(2)]
+    early = min(6, len(units))
     for n, unit in enumerate(units):
         product(*unit)
         if n == len(units) - 1:
             relay(1, 1)
-        for m in {1: (0, 1), 0: (), 2: ()}.get(n, (n - 1,)):
+        for m in {0: (), 1: (), 2: (), 3: (0, 1, 2, 3), 4: ()}.get(n, (n - 1,)):
             pair_sum(*units[m])
             if m < early:
-                reduce_first(*units[m])
-        if n == 1:
+                reduce_first(*units[m][:2], *units[m][3:])
+        if n == 3:
             arrived(chunks(na), a1r)
             pass_on(t, 0, 1)
             pass_on(t, 1, 1)
@@ -655,7 +659,7 @@
         dma, dma((nt,)), dma,
         dma((nt // 2,)), dma,
         dma, dma((nt,)),
-        dma, dma((2 * nt,)),
+        dma, dma((2 * nt + 2,)),
         dma, dma((nt, 2)),
         dma, dma((nt,)),
         dma, dma,

time: 80.3 us -> 79.8 us (level)
  no operation moved by 1% of the time
where the time goes in v7:
time: 79.8 us; the launch traced here: 79.7 us
  Pallas kernels  79 us (99%)
    pallas_call x1, Pallas kernels, body(): pl.pallas_call(functools.partial(kernel, ndp, nt, nqx), out_shape=(pltpu....  74.7 us
    pallas_call x1, Pallas kernels, body(): pl.pallas_call(write_out, out_shape=[jax.ShapeDtypeStruct(results[n].shap...  4.39 us

profile of v7, /device:TPU:0, one launch (start us, length us, event | category | flops | bytes accessed | tf_op | source)
XLA Modules:
  0.0 79.7 jit_solution(4692325222126858791)
XLA Ops:
  0.6 74.7 %shard_map.111 = (bf16[512,8192]{1,0:T(8,128)(2,1)S(1)}, bf16[512,8192]{1,0:T(8,128)(2,1)S(1)}, f32[512,128]{1,0:T(8,128)S(1)}, bf16[4,128,2048]{2,1,0:T(8,128)(...) custom-call(bf16[512,8192]{1,0:T(8,128)(2,1)} %x_hbm.1, bf16[512,512]{1,0:T(8,128)(2,1)} %kg_hbm.1, ...), custom_call_target="tpu_custom_call" | custom-call | tf_op jit(solution)/shard_map/pallas_call | solution.py:671
  75.3 4.4 %shard_map.112 = (bf16[512,8192]{1,0:T(8,128)(2,1)}, bf16[4,128,2048]{2,1,0:T(8,128)(2,1)}, f32[64,2048]{1,0:T(8,128)}, f32[64,2048]{1,0:T(8,128)}) custom-call(bf16[512,8192]{1,0:T(8,128)(2,1)S(1)} %get-tuple-element.14.grad, bf16[512,8192]{1,0:T(8,128)(2,1)S(1)} %get-tuple-element.15.x, f32[512,128]{1,0:T(8,128)S(1)} %get-tuple-element.16.down, ...), custom_call_target="tpu_custom_call" | custom-call | tf_op jit(solution)/shard_map/pallas_call | solution.py:692

commit v8 on v7

--- a/solution.py
+++ b/solution.py
@@ -459,20 +459,19 @@
     final(nt - 1)
     arrived(rz, zr)
 
-    nsend[...] = jnp.zeros_like(nsend)
-
-    @pl.loop(0, rows // 16)
-    def _(g):
-        r = pl.ds(pl.multiple_of(g * 16, 16), 16)
-        a = gsum[r, :]
-        for i in range(nt - 1):
-            a = a + rz[i, r, :].astype(F32)
-        gsum[r, :] = a
-        a = a * a
-        total = a[:, :128]
-        for k in range(1, cols // 128):
-            total = total + a[:, k * 128 : (k + 1) * 128]
-        nsend[...] += jnp.sum(total, axis=0, keepdims=True)
+    wide = min(512, cols)
+    squares = jnp.zeros((16, 128), F32)
+    for g in range(rows // 16):
+        for part in range(cols // wide):
+            r, col = slice(g * 16, (g + 1) * 16), slice(part * wide, (part + 1) * wide)
+            a = gsum[r, col]
+            for i in range(nt - 1):
+                a = a + rz[i, r, col].astype(F32)
+            gsum[r, col] = a
+            a = a * a
+            for k in range(wide // 128):
+                squares = squares + a[:, k * 128 : (k + 1) * 128]
+    nsend[...] = jnp.sum(squares, axis=0, keepdims=True)
 
     n = 0
     for b in reversed(range(nt)):
@@ -503,15 +502,18 @@
     def _(g):
         r = pl.ds(pl.multiple_of(g * 16, 16), 16)
         wr_ = pl.ds(pl.multiple_of(mine + q * rows + g * 16, 16), 16)
-        clipped = gsum[r, :] * clip
-        new_first = beta_one * m1[r, :] + (1.0 - beta_one) * clipped
-        new_second = beta_two * m2[r, :] + (1.0 - beta_two) * clipped * clipped
-        nf[r, :] = new_first
-        ns[r, :] = new_second
-        nwb[q, pl.ds(pl.multiple_of(nat + g * 16, 16), 16), :] = (
-            wf[t, wr_, :].astype(F32) * (1.0 - learn_rate * decay_rate)
-            - learn_rate * new_first / (jnp.sqrt(new_second) + eps_adam)
-        ).astype(BF16)
+        to = pl.ds(pl.multiple_of(nat + g * 16, 16), 16)
+        for part in range(cols // wide):
+            col = slice(part * wide, (part + 1) * wide)
+            clipped = gsum[r, col] * clip
+            new_first = beta_one * m1[r, col] + (1.0 - beta_one) * clipped
+            new_second = beta_two * m2[r, col] + (1.0 - beta_two) * clipped * clipped
+            nf[r, col] = new_first
+            ns[r, col] = new_second
+            nwb[q, to, col] = (
+                wf[t, wr_, col].astype(F32) * (1.0 - learn_rate * decay_rate)
+                - learn_rate * new_first / (jnp.sqrt(new_second) + eps_adam)
+            ).astype(BF16)
 
     def piece_of(yy, xx, part):
         return nwb.at[yy * nqx + xx, pl.ds(nat, rows), part]

time: 79.8 us -> 79.8 us (level)
  no operation moved by 1% of the time
where the time goes in v8:
time: 79.8 us; the launch traced here: 79.6 us
  Pallas kernels  79 us (99%)
    pallas_call x1, Pallas kernels, body(): pl.pallas_call(functools.partial(kernel, ndp, nt, nqx), out_shape=(pltpu....  74.6 us
    pallas_call x1, Pallas kernels, body(): pl.pallas_call(write_out, out_shape=[jax.ShapeDtypeStruct(results[n].shap...  4.39 us

profile of v8, /device:TPU:0, one launch (start us, length us, event | category | flops | bytes accessed | tf_op | source)
XLA Modules:
  0.0 79.6 jit_solution(5074850886640288433)
XLA Ops:
  0.6 74.6 %shard_map.111 = (bf16[512,8192]{1,0:T(8,128)(2,1)S(1)}, bf16[512,8192]{1,0:T(8,128)(2,1)S(1)}, f32[512,128]{1,0:T(8,128)S(1)}, bf16[4,128,2048]{2,1,0:T(8,128)(...) custom-call(bf16[512,8192]{1,0:T(8,128)(2,1)} %x_hbm.1, bf16[512,512]{1,0:T(8,128)(2,1)} %kg_hbm.1, ...), custom_call_target="tpu_custom_call" | custom-call | tf_op jit(solution)/shard_map/pallas_call | solution.py:673
  75.3 4.4 %shard_map.112 = (bf16[512,8192]{1,0:T(8,128)(2,1)}, bf16[4,128,2048]{2,1,0:T(8,128)(2,1)}, f32[64,2048]{1,0:T(8,128)}, f32[64,2048]{1,0:T(8,128)}) custom-call(bf16[512,8192]{1,0:T(8,128)(2,1)S(1)} %get-tuple-element.14.grad, bf16[512,8192]{1,0:T(8,128)(2,1)S(1)} %get-tuple-element.15.x, f32[512,128]{1,0:T(8,128)S(1)} %get-tuple-element.16.down, ...), custom_call_target="tpu_custom_call" | custom-call | tf_op jit(solution)/shard_map/pallas_call | solution.py:694

commit v9 on v7

--- a/solution.py
+++ b/solution.py
@@ -117,11 +117,11 @@
     kg_in = local(kg_hbm, kg, isem.at[1])
     pos_in = local(pos_hbm, pos, isem.at[2])
     freq_in = local(freq_hbm, freq, isem.at[3])
+    gain_copy = local(gain_hbm, gain_in, isem.at[4])
     x_in = []
     for k in range(ntile):
         piece = pl.ds(k * tile, tile)
         x_in.append(local(x_hbm.at[piece], x.at[piece], xsem.at[k]))
-    gain_copy = local(gain_hbm, gain_in, isem.at[4])
     m1_in = local(m1_hbm, m1, isem.at[5])
     m2_in = local(m2_hbm, m2, isem.at[6])
 
@@ -241,6 +241,10 @@
         remote(part, part, a3s, a3r.at[i], (mate, t))
 
     sent.append((wg.at[:, pl.ds(0, half)], a3s))
+
+    gain_copy.wait()
+    for k in range(width // 128):
+        gain[:, k * 128 : (k + 1) * 128] = gain_in[k : k + 1, :].astype(F32)
 
     cross[...] = jnp.zeros_like(cross)
     kg_in.wait()
@@ -285,10 +289,6 @@
 
     for k in range(ntile):
         sum_squares(k)
-
-    gain_copy.wait()
-    for k in range(width // 128):
-        gain[:, k * 128 : (k + 1) * 128] = gain_in[k : k + 1, :].astype(F32)
 
     sent.append((wg.at[:, pl.ds(0, half)], cs))
 

time: 79.8 us -> 79.7 us (level)
  no operation moved by 1% of the time
where the time goes in v9:
time: 79.7 us; the launch traced here: 79.5 us
  Pallas kernels  78.9 us (99%)
    pallas_call x1, Pallas kernels, body(): pl.pallas_call(functools.partial(kernel, ndp, nt, nqx), out_shape=(pltpu....  74.5 us
    pallas_call x1, Pallas kernels, body(): pl.pallas_call(write_out, out_shape=[jax.ShapeDtypeStruct(results[n].shap...  4.39 us

profile of v9, /device:TPU:0, one launch (start us, length us, event | category | flops | bytes accessed | tf_op | source)
XLA Modules:
  0.0 79.5 jit_solution(61289071745077538)
XLA Ops:
  0.6 74.5 %shard_map.111 = (bf16[512,8192]{1,0:T(8,128)(2,1)S(1)}, bf16[512,8192]{1,0:T(8,128)(2,1)S(1)}, f32[512,128]{1,0:T(8,128)S(1)}, bf16[4,128,2048]{2,1,0:T(8,128)(...) custom-call(bf16[512,8192]{1,0:T(8,128)(2,1)} %x_hbm.1, bf16[512,512]{1,0:T(8,128)(2,1)} %kg_hbm.1, ...), custom_call_target="tpu_custom_call" | custom-call | tf_op jit(solution)/shard_map/pallas_call | solution.py:671
  75.1 4.4 %shard_map.112 = (bf16[512,8192]{1,0:T(8,128)(2,1)}, bf16[4,128,2048]{2,1,0:T(8,128)(2,1)}, f32[64,2048]{1,0:T(8,128)}, f32[64,2048]{1,0:T(8,128)}) custom-call(bf16[512,8192]{1,0:T(8,128)(2,1)S(1)} %get-tuple-element.14.grad, bf16[512,8192]{1,0:T(8,128)(2,1)S(1)} %get-tuple-element.15.x, f32[512,128]{1,0:T(8,128)S(1)} %get-tuple-element.16.down, ...), custom_call_target="tpu_custom_call" | custom-call | tf_op jit(solution)/shard_map/pallas_call | solution.py:692
